TPU v7x, 32 devices: a whole 2x2x4 slice. The times are simulated.
32 devices in a mesh: groups: 2 (over y), wide: 4 (over z), narrow: 4 (over x, core).
Axes of the slice: x: 2, y: 2, z: 4, core: 2. Of those that a mesh axis runs over, the one named last changes fastest.
Arguments:
- hidden: bfloat16 [4096, 4096], P(('groups', 'wide')), parts along dimension 0, may hold values from -16 to 16
- w_qkv: bfloat16 [4096, 3, 2048], P('wide', None, 'narrow'), may hold values from -0.09375 to 0.09375
- w_out: bfloat16 [2048, 4096], P(None, 'wide'), may hold values from -0.125 to 0.125
- seg_ids: int32 [4096], P('groups'), parts along dimension 0, may hold values from 0 to 3, never falling along the last dimension, each value on 1 to 1024 neighbouring positions
- shift_heads: int32 [16], replicated, may hold values from 0 to 1, as said below
Outputs:
- layer_out: bfloat16 [4096, 4096], P(('groups', 'wide', 'narrow')), parts along dimension 0
There are 2 independent parts, one for each index of `groups`. A program takes and returns all parts, laid end to end along the dimension named above; an argument that names none is the same for every part. Nothing has to cross between parts.
Inputs may be any that keep to these rules, and one draw needn't show every extreme that they name: `shift_heads`: exactly half of the heads are marked with 1, the others with 0. `seg_ids`: never falls along the window; every number occurs on 1 to 1024 consecutive tokens, one on exactly that many.
All inputs are finite; a program needn't handle non-finite values.
Results may differ from a plain program's by a relative error of at most 0.012.
Values may be sent and summed in bfloat16 or wider, within the bound.
A program may use at most 128 MiB of HBM per device.

v0:
```python
import functools
import math

import jax
import jax.numpy as jnp
from jax import lax
from jax.experimental import pallas as pl
from jax.experimental.pallas import tpu as pltpu
from jax.sharding import PartitionSpec as P

HEAD_DIM = 128
GROUP = 512
SHIFT = 256

masked_out = -1e30
MESH = pl.DeviceIdType.MESH
ROWS = 128
WO_CHUNKS = 4


def layer_kernel(
    n, narrow, chunks, wo_chunks,
    hidden_ref, wq_ref, wo_ref, segq_ref, segk_ref, out_ref,
    wbuf, acc, wo_buf, q_buf, kv_buf, att, part, pair_in, pair_sum, far_in,
    own_sem,
    qs_r, qs_l, qr, qs_y, qr_y,
    os_r, os_l, o_r, os_y, or_y,
    kv_sem, pair_s, pair_r, far_s, far_r,
):
    me = lax.axis_index("wide")
    y = lax.axis_index("groups")
    spot = lax.axis_index("narrow")
    other = 1 - y
    across_n = narrow // 2
    high, low = spot // 2, lax.rem(spot, 2)
    depth = wq_ref.shape[1]
    half = wbuf.shape[3]
    tok = hidden_ref.shape[0]
    rows = depth // chunks
    steps = (n - 1) * chunks
    wo_rows = wo_buf.shape[2] // wo_chunks
    cols = wo_buf.shape[3]
    blocks = tok // SHIFT
    per_half = half // HEAD_DIM
    has_left, has_right = me > 0, me < n - 1
    right, left = {"wide": me + 1}, {"wide": me - 1}
    after, before = {"wide": lax.rem(me + 1, n)}, {"wide": lax.rem(me + n - 1, n)}
    opposite = {"groups": other}
    pair = {"narrow": high * 2 + 1 - low}
    far = [{"narrow": lax.rem(high + d, across_n) * 2 + low} for d in range(1, across_n)]
    far_from = [{"narrow": lax.rem(high + across_n - d, across_n) * 2 + low} for d in range(1, across_n)]

    barrier = pltpu.get_barrier_semaphore()
    greeted = [after, before, opposite, pair] + far
    for device in greeted:
        pl.semaphore_signal(barrier, inc=1, device_id=device, device_id_type=MESH)

    def w_at(shard, part_of, c):
        start = pl.multiple_of(shard * depth + c * rows, rows)
        return wbuf.at[part_of, :, pl.ds(start, rows)]

    def wq_own(c):
        return wq_ref.at[
            :, pl.ds(pl.multiple_of(c * rows, rows), rows), pl.ds(pl.multiple_of(y * half, half), half)
        ]

    def o_at(shard, part_of, c):
        return wo_buf.at[shard, part_of, pl.ds(pl.multiple_of(c * wo_rows, wo_rows), wo_rows)]

    def wo_own(c):
        return wo_ref.at[spot, y, pl.ds(pl.multiple_of(c * wo_rows, wo_rows), wo_rows)]

    def remote(src, dst, send, recv, device):
        return pltpu.make_async_remote_copy(
            src_ref=src, dst_ref=dst, send_sem=send, recv_sem=recv,
            device_id=device, device_id_type=MESH,
        )

    def q_right(shard, c, src=None):
        dst = w_at(shard, y, c)
        return remote(dst if src is None else src, dst, qs_r.at[shard, c], qr.at[shard, c], right)

    def q_left(shard, c, src=None):
        dst = w_at(shard, y, c)
        return remote(dst if src is None else src, dst, qs_l.at[shard, c], qr.at[shard, c], left)

    def q_across(shard, c, part_of):
        ref = w_at(shard, part_of, c)
        return remote(ref, ref, qs_y.at[shard, c], qr_y.at[shard, c], opposite)

    def o_right(shard, c, src=None):
        dst = o_at(shard, y, c)
        return remote(dst if src is None else src, dst, os_r.at[shard, c], o_r.at[shard, c], right)

    def o_left(shard, c, src=None):
        dst = o_at(shard, y, c)
        return remote(dst if src is None else src, dst, os_l.at[shard, c], o_r.at[shard, c], left)

    def o_across(shard, c, part_of):
        ref = o_at(shard, part_of, c)
        return remote(ref, ref, os_y.at[shard, c], or_y.at[shard, c], opposite)

    own = [
        pltpu.make_async_copy(
            wq_ref.at[:, :, pl.ds(h * half, half)],
            wbuf.at[h, :, pl.ds(pl.multiple_of(me * depth, depth), depth)],
            own_sem.at[h],
        )
        for h in range(2)
    ]
    own.append(pltpu.make_async_copy(wo_ref.at[spot], wo_buf.at[me], own_sem.at[2]))
    for copy in own:
        copy.start()
    pl.semaphore_wait(barrier, len(greeted))

    @pl.loop(0, chunks)
    def _(c):
        @pl.when(has_right)
        def _():
            q_right(me, c, wq_own(c)).start()

        @pl.when(has_left)
        def _():
            q_left(me, c, wq_own(c)).start()

    acc[...] = jnp.zeros_like(acc)
    own[0].wait()
    own[1].wait()

    def add(shard, part_of, c):
        start = pl.multiple_of(shard * depth + c * rows, rows)
        piece = hidden_ref[:, pl.ds(start, rows)]
        for i in range(3):
            acc[part_of, i] += jnp.dot(
                piece, wbuf[part_of, i, pl.ds(start, rows)], preferred_element_type=jnp.float32
            )

    @pl.loop(0, 2 * chunks)
    def _(i):
        add(me, i // chunks, lax.rem(i, chunks))

    def add_across(t):
        s, c = t // chunks, lax.rem(t, chunks)
        for there, shard in ((me - 1 - s >= 0, me - 1 - s), (me + 1 + s <= n - 1, me + 1 + s)):
            @pl.when(there)
            def _():
                q_across(shard, c, other).wait_recv()
                add(shard, other, c)

    def send_own_wo():
        @pl.loop(0, wo_chunks)
        def _(c):
            @pl.when(has_right)
            def _():
                o_right(me, c, wo_own(c)).start()

            @pl.when(has_left)
            def _():
                o_left(me, c, wo_own(c)).start()

    @pl.loop(0, steps)
    def _(t):
        s, c = t // chunks, lax.rem(t, chunks)

        @pl.when(t == steps - chunks)
        def _():
            send_own_wo()

        @pl.when(me - 1 - s >= 0)
        def _():
            q_right(me - 1 - s, c).wait_recv()

            @pl.when(has_right)
            def _():
                q_right(me - 1 - s, c).start()

            q_across(me - 1 - s, c, y).start()

        @pl.when(me + 1 + s <= n - 1)
        def _():
            q_left(me + 1 + s, c).wait_recv()

            @pl.when(has_left)
            def _():
                q_left(me + 1 + s, c).start()

            q_across(me + 1 + s, c, y).start()

        for there, shard in ((me - 1 - s >= 0, me - 1 - s), (me + 1 + s <= n - 1, me + 1 + s)):
            @pl.when(there)
            def _():
                add(shard, y, c)

        @pl.when(t > 0)
        def _():
            add_across(t - 1)

    add_across(steps - 1)
    for h in range(2):
        q_buf[h] = acc[h, 0].astype(jnp.bfloat16)
        for i in range(2):
            kv_buf[h, i, SHIFT:] = acc[h, 1 + i].astype(jnp.bfloat16)

    kv_copy = remote(
        kv_buf.at[:, :, pl.ds(tok, SHIFT)], kv_buf.at[:, :, pl.ds(0, SHIFT)],
        kv_sem.at[0], kv_sem.at[1], after,
    )
    kv_copy.start()

    causal = lax.broadcasted_iota(jnp.int32, (SHIFT, 2 * SHIFT), 1) <= (
        lax.broadcasted_iota(jnp.int32, (SHIFT, 2 * SHIFT), 0) + SHIFT
    )

    def attend(h, b):
        lanes = slice((h % per_half) * HEAD_DIM, (h % per_half + 1) * HEAD_DIM)
        mine, seen = slice(b * SHIFT, (b + 1) * SHIFT), slice(b * SHIFT, (b + 2) * SHIFT)
        keys, values = kv_buf.at[h // per_half, 0], kv_buf.at[h // per_half, 1]
        scores = lax.dot_general(
            q_buf[h // per_half, mine, lanes], keys[seen, lanes], (((1,), (1,)), ((), ())),
            preferred_element_type=jnp.float32,
        ) * (1.0 / math.sqrt(HEAD_DIM))
        allowed = causal & (segq_ref[mine, :] == segk_ref[h, b])
        scores = jnp.where(allowed, scores, masked_out)
        exponent = jnp.exp(scores - jnp.max(scores, axis=-1, keepdims=True))
        weights = exponent / jnp.sum(exponent, axis=-1, keepdims=True)
        att[mine, h * HEAD_DIM : (h + 1) * HEAD_DIM] = jnp.dot(
            weights.astype(jnp.bfloat16), values[seen, lanes], preferred_element_type=jnp.float32
        ).astype(jnp.bfloat16)

    least = jnp.minimum(me, n - 1 - me)

    def block_of(k):
        turn = (k + 1) // 2
        near = jnp.where(lax.rem(k, 2) == 1, me - turn, me + turn)
        rest = jnp.where(me > least, me - (k - least), me + (k - least))
        return jnp.where(k <= 2 * least, near, rest)

    def pass_on(k):
        shard = block_of(k)

        @pl.loop(0, wo_chunks)
        def _(c):
            o_right(shard, c).wait_recv()

            @pl.when(jnp.logical_and(shard < me, has_right))
            def _():
                o_right(shard, c).start()

            @pl.when(jnp.logical_and(shard > me, has_left))
            def _():
                o_left(shard, c).start()

            o_across(shard, c, y).start()

    def pair_copy(shard, a):
        return remote(
            part.at[shard, a * 2 + 1 - low], pair_in.at[shard, a],
            pair_s.at[shard, a], pair_r.at[shard, a], pair,
        )

    def far_copy(shard, d):
        a = lax.rem(high + d, across_n)
        return remote(
            pair_sum.at[shard, a], far_in.at[shard, d - 1],
            far_s.at[shard, d - 1], far_r.at[shard, d - 1], far[d - 1],
        )

    def far_arrival(shard, d):
        return remote(
            pair_sum.at[shard, high], far_in.at[shard, d - 1],
            far_s.at[shard, d - 1], far_r.at[shard, d - 1], far_from[d - 1],
        )

    def multiply(k):
        shard = block_of(k)
        width = att.shape[1] // 2
        share = tok // narrow
        for p in range(narrow):
            a_rows = att[p * share : (p + 1) * share, :]
            total = jnp.dot(a_rows[:, :width], wo_buf[shard, 0], preferred_element_type=jnp.float32)
            total += jnp.dot(a_rows[:, width:], wo_buf[shard, 1], preferred_element_type=jnp.float32)
            part[shard, p] = total.astype(jnp.bfloat16)
        for a in range(across_n):
            pair_copy(shard, a).start()

    def sum_pair(k):
        shard = block_of(k)
        for a in range(across_n):
            pair_copy(shard, a).wait_recv()
            total = part[shard, a * 2 + low].astype(jnp.float32) + pair_in[shard, a].astype(jnp.float32)
            pair_sum[shard, a] = total.astype(jnp.bfloat16)
        for d in range(1, across_n):
            far_copy(shard, d).start()

    def finish(k):
        shard = block_of(k)
        total = part[shard, high * 2 + low].astype(jnp.float32) + pair_in[shard, high].astype(jnp.float32)
        for d in range(1, across_n):
            far_arrival(shard, d).wait_recv()
            total += far_in[shard, d - 1].astype(jnp.float32)
        out_ref[:, pl.ds(pl.multiple_of(shard * cols, cols), cols)] = total.astype(out_ref.dtype)

    heads = 2 * per_half
    for b in range(1, blocks):
        for h in range(heads):
            attend(h, b)
    pass_on(1)
    pass_on(2)
    kv_copy.wait_recv()
    for h in range(heads):
        attend(h, 0)
    own[2].wait()
    multiply(0)

    @pl.loop(1, n)
    def _(k):
        @pl.when(k > 2)
        def _():
            pass_on(k)

        sum_pair(k - 1)

        @pl.when(k > 1)
        def _():
            finish(k - 2)

        shard = block_of(k)

        @pl.loop(0, wo_chunks)
        def _(c):
            o_across(shard, c, other).wait_recv()

        multiply(k)

    sum_pair(n - 1)
    finish(n - 2)
    finish(n - 1)

    kv_copy.wait_send()

    @pl.loop(0, n)
    def _(shard):
        for a in range(across_n):
            pair_copy(shard, a).wait_send()
        for d in range(1, across_n):
            far_copy(shard, d).wait_send()
        goes_right = jnp.logical_and(shard <= me, has_right)
        goes_left = jnp.logical_and(shard >= me, has_left)
        for count, to_right, to_left, to_other in (
            (chunks, q_right, q_left, q_across), (wo_chunks, o_right, o_left, o_across)
        ):
            @pl.loop(0, count)
            def _(c):
                @pl.when(goes_right)
                def _():
                    to_right(shard, c).wait_send()

                @pl.when(goes_left)
                def _():
                    to_left(shard, c).wait_send()

                @pl.when(shard != me)
                def _():
                    to_other(shard, c, y).wait_send()


def layer(hidden, wq, wo, seg_q, seg_k):
    n, narrow = lax.axis_size("wide"), lax.axis_size("narrow")
    tok, width = hidden.shape
    half = wq.shape[2] // 2
    chunks = max(1, wq.shape[1] // ROWS)
    wo_chunks = WO_CHUNKS
    cols = wo.shape[3]
    share = tok // narrow
    vmem = pl.BlockSpec(memory_space=pltpu.VMEM)
    hbm = pl.BlockSpec(memory_space=pl.ANY)
    dma = pltpu.SemaphoreType.DMA
    bf16 = jnp.bfloat16
    return pl.pallas_call(
        functools.partial(layer_kernel, n, narrow, chunks, wo_chunks),
        out_shape=jax.ShapeDtypeStruct((share, n * cols), bf16),
        in_specs=[vmem, hbm, hbm, vmem, vmem],
        out_specs=vmem,
        scratch_shapes=[
            pltpu.VMEM((2, 3, width, half), bf16),
            pltpu.VMEM((2, 3, tok, half), jnp.float32),
            pltpu.VMEM((n,) + wo.shape[1:], bf16),
            pltpu.VMEM((2, tok, half), bf16),
            pltpu.VMEM((2, 2, tok + SHIFT, half), bf16),
            pltpu.VMEM((tok, 2 * half), bf16),
            pltpu.VMEM((n, narrow, share, cols), bf16),
            pltpu.VMEM((n, narrow // 2, share, cols), bf16),
            pltpu.VMEM((n, narrow // 2, share, cols), bf16),
            pltpu.VMEM((n, max(1, narrow // 2 - 1), share, cols), bf16),
            dma((3,)),
        ]
        + [dma((n, chunks))] * 5
        + [dma((n, wo_chunks))] * 5
        + [dma((2,))]
        + [dma((n, narrow // 2))] * 2
        + [dma((n, max(1, narrow // 2 - 1)))] * 2,
        compiler_params=pltpu.CompilerParams(
            collective_id=0, has_side_effects=True, vmem_limit_bytes=58 * 1024 * 1024
        ),
    )(hidden, wq, wo, seg_q, seg_k)


def per_device(hidden, w_qkv, w_out, seg_ids, shift_heads):
    tok_rows = hidden.shape[0]
    local_f = w_qkv.shape[2]
    heads_here = local_f // HEAD_DIM
    blocks = tok_rows // SHIFT
    narrow = lax.axis_size("narrow")
    first_tok = lax.axis_index("wide") * tok_rows
    shifted = lax.dynamic_slice_in_dim(shift_heads, lax.axis_index("narrow") * heads_here, heads_here) > 0

    doubled = jnp.concatenate([seg_ids[-SHIFT:], seg_ids], 0)
    seg_here = lax.dynamic_slice_in_dim(doubled, first_tok, tok_rows + SHIFT)
    seg_q = seg_here[SHIFT:, None]
    windows = jnp.stack([seg_here[b * SHIFT : (b + 2) * SHIFT] for b in range(blocks)])
    odd = (jnp.arange(blocks) % 2 == 1)[None, :, None]
    reaches = (shifted[:, None, None] != odd) | (jnp.arange(2 * SHIFT) >= SHIFT)[None, None, :]
    seg_k = jnp.where(reaches, windows[None], -1)[:, :, None, :]

    wq = w_qkv.transpose(1, 0, 2)
    wo = w_out.reshape(narrow, 2, local_f // 2, -1)
    return layer(hidden, wq, wo, seg_q, seg_k)


def solution(mesh):
    placed = (
        P(("groups", "wide"), None),
        P("wide", None, "narrow"),
        P(None, "wide"),
        P("groups"),
        P(),
    )
    return jax.shard_map(
        per_device,
        mesh=mesh,
        in_specs=placed,
        out_specs=P(("groups", "wide", "narrow"), None),
        check_vma=False,
    )
```

profile of v0, /device:TPU:1, one launch (start us, length us, event | category | flops | bytes accessed | tf_op | source)
XLA Modules:
  0.0 187.4 jit_solution(9049819380262095379)
XLA Ops:
  0.0 0.7 dynamic-slice_compare_fusion
  0.7 0.1 broadcast_compare_fusion
  0.8 0.7 slice.10
  1.5 0.8 fusion
  2.3 0.7 or_select_fusion.segk_ref
  3.0 0.9 copy.6.segq_ref
  3.8 181.3 %shard_map.55 = bf16[128,4096]{1,0:T(8,128)(2,1)} custom-call(bf16[512,4096]{1,0:T(8,128)(2,1)} %hidden_ref.1, bf16[3,1024,512]{2,1,0:T(8,128)(2,1)} %bitcast.6, bf16[4,2,256,1024]{3,2,1,0:T(8,128)(2,1)} %bitcast.5, s32[512,1]{1,0:T(8,128)} %copy.6.segq_ref, s32[4,2,1,512]{3,2,1,0:T(1,128)} %or_select_fusion.segk_ref), custom_call_target="tpu_custom_call" | custom-call | tf_op jit(solution)/shard_map/pallas_call | solution.py:379
  185.1 2.3 %copy.8 = bf16[128,4096]{1,0:T(8,128)(2,1)} copy(bf16[128,4096]{1,0:T(8,128)(2,1)} %shard_map.55) | data formatting | bytes 2097152
  (4 shorter events, 0.0 us)
where the time goes:
time: 190 us; the launch traced here: 187 us
  Pallas kernels  181 us (95%)
  local copies, waits for them, and re-layouts  3.84 us (2%)
  other arithmetic  2.29 us (1%)
    pallas_call x1, Pallas kernels, layer(): pl.pallas_call(functools.partial(layer_kernel, n, narrow, chunks, wo_chun...  181 us

commit v1 on v0

--- a/solution.py
+++ b/solution.py
@@ -16,6 +16,7 @@
 MESH = pl.DeviceIdType.MESH
 ROWS = 128
 WO_CHUNKS = 4
+DIRECT = 5
 
 
 def layer_kernel(
@@ -427,6 +428,591 @@
     return layer(hidden, wq, wo, seg_q, seg_k)
 
 
+def hub_kernel(
+    chunks, wo_chunks, direct,
+    hidden_ref, wq_ref, wo_ref, segq_ref, segk_ref, out_ref,
+    wbuf, hid, acc, q_buf, kv_buf, att, wo_buf, stage,
+    own_sem, he_s, he_r, hx_s, hx_r, hc_s, hc_r,
+    wm_s, wm_r, we_s, we_r, wy_s, wy_r, kv_sem,
+    om_s, om_r, oe_s, oe_r, oy_s, oy_r,
+    ax_s, ax_r, ac_s, ac_r, res_s, res_r,
+):
+    n, narrow = lax.axis_size("wide"), lax.axis_size("narrow")
+    me = lax.axis_index("wide")
+    y = lax.axis_index("groups")
+    spot = lax.axis_index("narrow")
+    opp = 1 - y
+    side = me // (n // 2)
+    inner, outer = n // 2 - 1 + side, side * (n - 1)
+    far_inner, far_outer = n - 1 - inner, n - 1 - outer
+    is_inner, is_outer = me == inner, me == outer
+    high, low = spot // 2, lax.rem(spot, 2)
+    core_n, x_n = high * 2 + 1 - low, (1 - high) * 2 + low
+    diag_n = (1 - high) * 2 + 1 - low
+    depth = wq_ref.shape[1]
+    tok = hidden_ref.shape[0]
+    half = wbuf.shape[3]
+    rows = depth // chunks
+    pair_rows = 2 * rows
+    pairs = chunks // 2
+    quarter = tok // narrow
+    span = 2 * tok
+    blocks = span // SHIFT
+    own_pos = 1 - side
+    own_row = pl.multiple_of(own_pos * tok, tok)
+    far_row = pl.multiple_of(side * tok, tok)
+    wo_half, wo_cols = wo_buf.shape[2], wo_buf.shape[3]
+    wo_rows = wo_half // wo_chunks
+    cols = wo_ref.shape[1]
+    per_half = half // HEAD_DIM
+    heads = 2 * per_half
+    to_core, to_x, to_y = {"narrow": core_n}, {"narrow": x_n}, {"groups": opp}
+    to_far, to_inner = {"wide": far_inner}, {"wide": inner}
+
+    def remote(src, dst, send, recv, device):
+        return pltpu.make_async_remote_copy(
+            src_ref=src, dst_ref=dst, send_sem=send, recv_sem=recv,
+            device_id=device, device_id_type=MESH,
+        )
+
+    def w_at(shard, part, c):
+        start = pl.multiple_of(shard * depth + c * rows, rows)
+        return wbuf.at[part, :, pl.ds(start, rows)]
+
+    def wq_at(part, c):
+        return wq_ref.at[
+            :, pl.ds(pl.multiple_of(c * rows, rows), rows), pl.ds(pl.multiple_of(part * half, half), half)
+        ]
+
+    def o_at(shard, part, c):
+        return wo_buf.at[shard, part, pl.ds(pl.multiple_of(c * wo_rows, wo_rows), wo_rows)]
+
+    def wo_at(part, c):
+        start = pl.multiple_of(part * wo_half + c * wo_rows, wo_rows)
+        return wo_ref.at[pl.ds(start, wo_rows), pl.ds(pl.multiple_of(spot * wo_cols, wo_cols), wo_cols)]
+
+    def h_at(row_n, k):
+        start = pl.multiple_of(far_row + row_n * quarter, quarter)
+        return hid.at[pl.ds(start, quarter), pl.ds(pl.multiple_of(k * depth, depth), depth)]
+
+    def h_end(k):
+        src = hidden_ref.at[
+            pl.ds(pl.multiple_of(spot * quarter, quarter), quarter), pl.ds(pl.multiple_of(k * depth, depth), depth)
+        ]
+        return remote(src, h_at(spot, k), he_s.at[k], he_r.at[k], to_inner)
+
+    def h_x(k, row_n):
+        return remote(h_at(row_n, k), h_at(row_n, k), hx_s.at[k], hx_r.at[k], to_x)
+
+    def h_core(j, k, row_n):
+        return remote(h_at(row_n, k), h_at(row_n, k), hc_s.at[j, k], hc_r.at[j, k], to_core)
+
+    def w_end(j, c):
+        part = y if j == 0 else opp
+        return remote(wq_at(part, c), w_at(outer, part, c), we_s.at[j, c], we_r.at[j, c], to_inner)
+
+    def w_mid_send(s, c):
+        if s == 0:
+            return remote(wq_at(y, c), w_at(inner, y, c), wm_s.at[s, c], wm_r.at[s, c], to_far)
+        return remote(w_at(outer, y, c), w_at(outer, y, c), wm_s.at[s, c], wm_r.at[s, c], to_far)
+
+    def far_shard(s):
+        return jnp.where(s == 0, far_inner, far_outer)
+
+    def w_mid_recv(s, c):
+        ref = w_at(far_shard(s), y, c)
+        return remote(ref, ref, wm_s.at[s, c], wm_r.at[s, c], to_far)
+
+    def y_shard(s):
+        return jnp.where(s == 2, outer, far_shard(s))
+
+    def w_y(s, c, part):
+        ref = w_at(y_shard(s), part, c)
+        return remote(ref, ref, wy_s.at[s, c], wy_r.at[s, c], to_y)
+
+    def o_end(j, c):
+        part = y if j == 0 else opp
+        return remote(wo_at(part, c), o_at(outer, part, c), oe_s.at[j, c], oe_r.at[j, c], to_inner)
+
+    def o_mid_send(s, c):
+        if s == 0:
+            return remote(wo_at(y, c), o_at(inner, y, c), om_s.at[s, c], om_r.at[s, c], to_far)
+        return remote(o_at(outer, y, c), o_at(outer, y, c), om_s.at[s, c], om_r.at[s, c], to_far)
+
+    def o_mid_recv(s, c):
+        ref = o_at(far_shard(s), y, c)
+        return remote(ref, ref, om_s.at[s, c], om_r.at[s, c], to_far)
+
+    def o_y(s, c, part):
+        ref = o_at(far_shard(s), part, c)
+        return remote(ref, ref, oy_s.at[s, c], oy_r.at[s, c], to_y)
+
+    def att_at(row_n, b):
+        return att.at[row_n, pl.ds(b * SHIFT, SHIFT)]
+
+    def att_x(b, row_n):
+        return remote(att_at(row_n, b), att_at(row_n, b), ax_s.at[b], ax_r.at[b], to_x)
+
+    def att_core(j, b, row_n):
+        return remote(att_at(row_n, b), att_at(row_n, b), ac_s.at[j, b], ac_r.at[j, b], to_core)
+
+    def res_cols(shard, row_n):
+        return pl.ds(pl.multiple_of(shard * cols + row_n * wo_cols, wo_cols), wo_cols)
+
+    def result(shard, pos, to_n):
+        return remote(
+            stage.at[shard, pl.ds(pos * tok + to_n * quarter, quarter)],
+            out_ref.at[:, res_cols(shard, spot)],
+            res_s.at[shard, pos, to_n], res_r.at[shard, spot],
+            {"wide": side * (n // 2) + pos, "narrow": to_n},
+        )
+
+    def result_arrival(shard, from_n):
+        ref = out_ref.at[:, res_cols(shard, from_n)]
+        return remote(ref, ref, res_s.at[shard, 0, 0], res_r.at[shard, from_n], to_core)
+
+    kv_copy = remote(
+        kv_buf.at[:, :, pl.ds(span, SHIFT)], kv_buf.at[:, :, pl.ds(0, SHIFT)],
+        kv_sem.at[0], kv_sem.at[1], to_far,
+    )
+
+    barrier = pltpu.get_barrier_semaphore()
+
+    @pl.when(is_outer)
+    def _():
+        for p in range(narrow):
+            pl.semaphore_signal(barrier, inc=1, device_id={"wide": inner, "narrow": p}, device_id_type=MESH)
+        pl.semaphore_wait(barrier, narrow)
+
+        @pl.loop(0, n)
+        def _(k):
+            h_end(k).start()
+
+        @pl.loop(0, chunks)
+        def _(c):
+            w_end(0, c).start()
+
+        @pl.loop(0, direct)
+        def _(c):
+            w_end(1, c).start()
+
+        for j in range(2):
+            @pl.loop(0, wo_chunks)
+            def _(c):
+                o_end(j, c).start()
+
+        @pl.loop(0, n)
+        def _(k):
+            h_end(k).wait_send()
+
+        @pl.loop(0, chunks)
+        def _(c):
+            w_end(0, c).wait_send()
+
+        @pl.loop(0, direct)
+        def _(c):
+            w_end(1, c).wait_send()
+
+        for j in range(2):
+            @pl.loop(0, wo_chunks)
+            def _(c):
+                o_end(j, c).wait_send()
+
+        @pl.loop(0, n)
+        def _(shard):
+            for p in range(narrow):
+                result_arrival(shard, p).wait_recv()
+
+    @pl.when(is_inner)
+    def _():
+        own = [
+            pltpu.make_async_copy(
+                wq_ref.at[:, :, pl.ds(h * half, half)],
+                wbuf.at[h, :, pl.ds(pl.multiple_of(inner * depth, depth), depth)],
+                own_sem.at[h],
+            )
+            for h in range(2)
+        ]
+        own.append(pltpu.make_async_copy(hidden_ref, hid.at[pl.ds(own_row, tok)], own_sem.at[2]))
+        own += [
+            pltpu.make_async_copy(
+                wo_ref.at[pl.ds(h * wo_half, wo_half), pl.ds(pl.multiple_of(spot * wo_cols, wo_cols), wo_cols)],
+                wo_buf.at[inner, h],
+                own_sem.at[3 + h],
+            )
+            for h in range(2)
+        ]
+        for copy in own:
+            copy.start()
+        peers = [{"narrow": core_n}, {"narrow": x_n}, {"narrow": diag_n}, to_y, to_far]
+        peers += [{"wide": outer, "narrow": p} for p in range(narrow)]
+        for device in peers:
+            pl.semaphore_signal(barrier, inc=1, device_id=device, device_id_type=MESH)
+        pl.semaphore_wait(barrier, len(peers))
+
+        @pl.loop(0, chunks)
+        def _(c):
+            w_mid_send(0, c).start()
+
+        acc[...] = jnp.zeros_like(acc)
+
+        def add(row, size, shard, part, p):
+            start = pl.multiple_of(shard * depth + p * pair_rows, pair_rows)
+            piece = hid[pl.ds(row, size), pl.ds(start, pair_rows)]
+            for i in range(3):
+                acc[part, i, pl.ds(row, size)] += jnp.dot(
+                    piece, wbuf[part, i, pl.ds(start, pair_rows)], preferred_element_type=jnp.float32
+                )
+
+        for copy in own[:3]:
+            copy.wait()
+
+        @pl.loop(0, 2 * pairs)
+        def _(u):
+            add(own_row, tok, inner, u // pairs, lax.rem(u, pairs))
+
+        late = 3 * pairs // 4
+        catch_up = 2 * pairs + 2 * late
+
+        @pl.loop(0, 2 * chunks)
+        def _(t):
+            s, c = t // chunks, lax.rem(t, chunks)
+            w_mid_recv(s, c).wait_recv()
+            w_y(s, c, y).start()
+
+            first = chunks - 2
+
+            @pl.when(jnp.logical_and(t >= first, t < first + chunks))
+            def _():
+                w_end(0, t - first).wait_recv()
+                w_mid_send(1, t - first).start()
+
+            @pl.when(t == first + chunks)
+            def _():
+                @pl.loop(0, wo_chunks)
+                def _(k):
+                    o_mid_send(0, k).start()
+
+            @pl.when(jnp.logical_and(t >= 2, t < 2 + n))
+            def _():
+                h_end(t - 2).wait_recv()
+                h_x(t - 2, spot).start()
+                h_core(0, t - 2, spot).start()
+
+            @pl.when(jnp.logical_and(t >= 4, t < 4 + n))
+            def _():
+                h_x(t - 4, x_n).wait_recv()
+                h_core(1, t - 4, x_n).start()
+
+            @pl.when(t == chunks)
+            def _():
+                @pl.loop(0, n)
+                def _(k):
+                    h_core(0, k, core_n).wait_recv()
+                    h_core(1, k, diag_n).wait_recv()
+
+            @pl.when(t >= 2)
+            def _():
+                w_y((t - 2) // chunks, lax.rem(t - 2, chunks), opp).wait_recv()
+                even = lax.rem(t, 2) == 0
+                last = jnp.where(even, t - 1, t - 2)
+
+                @pl.when(last >= 1)
+                def _():
+                    shard = far_shard(last // chunks)
+                    part = jnp.where(even, y, opp)
+                    p = lax.rem(last, chunks) // 2
+                    add(own_row, tok, shard, part, p)
+
+                    @pl.when(t >= chunks)
+                    def _():
+                        add(far_row, tok, shard, part, p)
+
+            @pl.when(t >= chunks)
+            def _():
+                @pl.when(lax.rem(t, 2) == 1)
+                def _():
+                    @pl.loop(0, 2)
+                    def _(k):
+                        add(pl.multiple_of(k * tok, tok), tok, outer, y, (t - chunks - 1) // 2)
+
+                u0 = 2 * (t - chunks)
+
+                @pl.loop(u0, jnp.minimum(u0 + 2, catch_up))
+                def _(u):
+                    own_done = u < 2 * pairs
+                    v = u - 2 * pairs
+                    shard = jnp.where(own_done, inner, far_inner)
+                    part = jnp.where(own_done, u // pairs, jnp.where(v < late, y, opp))
+                    p = jnp.where(own_done, lax.rem(u, pairs), lax.rem(v + 2 * late, late))
+                    add(far_row, tok, shard, part, p)
+
+        @pl.loop(direct, chunks)
+        def _(c):
+            w_y(2, c, y).start()
+
+        def add_all(shard, part, p):
+            add(0, span, shard, part, p)
+
+        add_all(far_outer, y, pairs - 1)
+
+        @pl.loop(0, 2)
+        def _(k):
+            w_y(1, chunks - 2 + k, opp).wait_recv()
+
+        add_all(far_outer, opp, pairs - 1)
+
+        @pl.loop(0, pairs)
+        def _(p):
+            for k in range(2):
+                c = 2 * p + k
+
+                @pl.when(c < direct)
+                def _():
+                    w_end(1, c).wait_recv()
+
+                @pl.when(c >= direct)
+                def _():
+                    w_y(2, c, opp).wait_recv()
+
+            add_all(outer, opp, p)
+
+        for h in range(2):
+            for i in range(2):
+                kv_buf[h, i, SHIFT:] = acc[h, 1 + i].astype(jnp.bfloat16)
+        kv_copy.start()
+        for h in range(2):
+            q_buf[h] = acc[h, 0].astype(jnp.bfloat16)
+
+        causal = lax.broadcasted_iota(jnp.int32, (SHIFT, 2 * SHIFT), 1) <= (
+            lax.broadcasted_iota(jnp.int32, (SHIFT, 2 * SHIFT), 0) + SHIFT
+        )
+
+        def attend(b):
+            for h in range(heads):
+                lanes = slice((h % per_half) * HEAD_DIM, (h % per_half + 1) * HEAD_DIM)
+                mine, seen = slice(b * SHIFT, (b + 1) * SHIFT), slice(b * SHIFT, (b + 2) * SHIFT)
+                keys, values = kv_buf.at[h // per_half, 0], kv_buf.at[h // per_half, 1]
+                scores = lax.dot_general(
+                    q_buf[h // per_half, mine, lanes], keys[seen, lanes], (((1,), (1,)), ((), ())),
+                    preferred_element_type=jnp.float32,
+                ) * (1.0 / math.sqrt(HEAD_DIM))
+                allowed = causal & (segq_ref[mine, :] == segk_ref[h, b])
+                scores = jnp.where(allowed, scores, masked_out)
+                exponent = jnp.exp(scores - jnp.max(scores, axis=-1, keepdims=True))
+                weights = exponent / jnp.sum(exponent, axis=-1, keepdims=True)
+                att[spot, mine, h * HEAD_DIM : (h + 1) * HEAD_DIM] = jnp.dot(
+                    weights.astype(jnp.bfloat16), values[seen, lanes], preferred_element_type=jnp.float32
+                ).astype(jnp.bfloat16)
+            att_x(b, spot).start()
+            att_core(0, b, spot).start()
+
+        def relay(b):
+            att_x(b, x_n).wait_recv()
+            att_core(1, b, x_n).start()
+
+        def gathered(b):
+            att_core(0, b, core_n).wait_recv()
+            att_core(1, b, diag_n).wait_recv()
+
+        def multiply(shard, b):
+            total = None
+            for p in range(narrow):
+                a_cols = att.shape[2]
+                start = (p % (narrow // 2)) * a_cols
+                term = jnp.dot(
+                    att[p, b * SHIFT : (b + 1) * SHIFT],
+                    wo_buf[shard, p // (narrow // 2), start : start + a_cols],
+                    preferred_element_type=jnp.float32,
+                )
+                total = term if total is None else total + term
+            done = total.astype(jnp.bfloat16)
+            stage[shard, b * SHIFT : (b + 1) * SHIFT] = done
+            pos = b * SHIFT // tok
+            for k in range(SHIFT // quarter):
+                to_n = b * SHIFT % tok // quarter + k
+                here = jnp.logical_and(pos == own_pos, spot == to_n)
+
+                @pl.when(here)
+                def _():
+                    out_ref[:, res_cols(shard, spot)] = done[k * quarter : (k + 1) * quarter]
+
+                @pl.when(jnp.logical_not(here))
+                def _():
+                    result(shard, pos, to_n).start()
+
+        @pl.loop(0, wo_chunks)
+        def _(c):
+            o_mid_recv(0, c).wait_recv()
+            o_y(0, c, y).start()
+
+        def forward_wo(c):
+            o_end(0, c).wait_recv()
+            o_mid_send(1, c).start()
+
+        attend(1)
+        for c in range(0, wo_chunks // 2):
+            forward_wo(c)
+        attend(2)
+        relay(1)
+        for c in range(wo_chunks // 2, wo_chunks):
+            forward_wo(c)
+        attend(3)
+        relay(2)
+        for copy in own[3:]:
+            copy.wait()
+        gathered(1)
+        multiply(inner, 1)
+        relay(3)
+        gathered(2)
+        multiply(inner, 2)
+        gathered(3)
+        multiply(inner, 3)
+        kv_copy.wait_recv()
+        attend(0)
+
+        @pl.loop(0, wo_chunks)
+        def _(c):
+            o_y(0, c, opp).wait_recv()
+
+        for b in range(1, blocks):
+            multiply(far_inner, b)
+        relay(0)
+
+        @pl.loop(0, wo_chunks)
+        def _(c):
+            o_mid_recv(1, c).wait_recv()
+            o_y(1, c, y).start()
+
+        gathered(0)
+        multiply(inner, 0)
+        multiply(far_inner, 0)
+
+        @pl.loop(0, wo_chunks)
+        def _(c):
+            o_end(1, c).wait_recv()
+
+        for b in range(blocks):
+            multiply(outer, b)
+
+        @pl.loop(0, wo_chunks)
+        def _(c):
+            o_y(1, c, opp).wait_recv()
+
+        for b in range(blocks):
+            multiply(far_outer, b)
+
+        @pl.loop(0, n)
+        def _(shard):
+            for p in range(narrow):
+                @pl.when(spot != p)
+                def _():
+                    result_arrival(shard, p).wait_recv()
+
+        @pl.loop(0, n)
+        def _(k):
+            h_x(k, spot).wait_send()
+            h_core(0, k, spot).wait_send()
+            h_core(1, k, x_n).wait_send()
+
+        @pl.loop(0, chunks)
+        def _(c):
+            w_mid_send(0, c).wait_send()
+            w_mid_send(1, c).wait_send()
+            w_y(0, c, y).wait_send()
+            w_y(1, c, y).wait_send()
+
+        @pl.loop(direct, chunks)
+        def _(c):
+            w_y(2, c, y).wait_send()
+
+        kv_copy.wait_send()
+
+        @pl.loop(0, wo_chunks)
+        def _(c):
+            o_mid_send(0, c).wait_send()
+            o_mid_send(1, c).wait_send()
+            o_y(0, c, y).wait_send()
+            o_y(1, c, y).wait_send()
+
+        for b in range(blocks):
+            att_x(b, spot).wait_send()
+            att_core(0, b, spot).wait_send()
+            att_core(1, b, x_n).wait_send()
+
+        @pl.loop(0, n)
+        def _(shard):
+            for pos in range(2):
+                for to_n in range(narrow):
+                    @pl.when(jnp.logical_not(jnp.logical_and(pos == own_pos, spot == to_n)))
+                    def _():
+                        result(shard, pos, to_n).wait_send()
+
+
+def hub_layer(hidden, wq, wo, seg_q, seg_k):
+    n, narrow = lax.axis_size("wide"), lax.axis_size("narrow")
+    tok, width = hidden.shape
+    half = wq.shape[2] // 2
+    chunks = wq.shape[1] // ROWS
+    wo_chunks = WO_CHUNKS
+    direct = DIRECT
+    cols = wo.shape[1]
+    wo_half, wo_cols = wo.shape[0] // 2, cols // narrow
+    quarter, span = tok // narrow, 2 * tok
+    blocks = span // SHIFT
+    vmem = pl.BlockSpec(memory_space=pltpu.VMEM)
+    hbm = pl.BlockSpec(memory_space=pl.ANY)
+    dma = pltpu.SemaphoreType.DMA
+    bf16 = jnp.bfloat16
+    return pl.pallas_call(
+        functools.partial(hub_kernel, chunks, wo_chunks, direct),
+        out_shape=jax.ShapeDtypeStruct((quarter, n * cols), bf16),
+        in_specs=[hbm, hbm, hbm, vmem, vmem],
+        out_specs=vmem,
+        scratch_shapes=[
+            pltpu.VMEM((2, 3, width, half), bf16),
+            pltpu.VMEM((span, width), bf16),
+            pltpu.VMEM((2, 3, span, half), jnp.float32),
+            pltpu.VMEM((2, span, half), bf16),
+            pltpu.VMEM((2, 2, span + SHIFT, half), bf16),
+            pltpu.VMEM((narrow, span, 2 * half), bf16),
+            pltpu.VMEM((n, 2, wo_half, wo_cols), bf16),
+            pltpu.VMEM((n, span, wo_cols), bf16),
+            dma((5,)),
+        ]
+        + [dma((n,))] * 4
+        + [dma((2, n))] * 2
+        + [dma((2, chunks))] * 4
+        + [dma((3, chunks))] * 2
+        + [dma((2,))]
+        + [dma((2, wo_chunks))] * 6
+        + [dma((blocks,))] * 2
+        + [dma((2, blocks))] * 2
+        + [dma((n, 2, narrow)), dma((n, narrow))],
+        compiler_params=pltpu.CompilerParams(
+            collective_id=0, has_side_effects=True, vmem_limit_bytes=58 * 1024 * 1024
+        ),
+    )(hidden, wq, wo, seg_q, seg_k)
+
+
+def hub_per_device(hidden, w_qkv, w_out, seg_ids, shift_heads):
+    n = lax.axis_size("wide")
+    heads_here = w_qkv.shape[2] // HEAD_DIM
+    span = hidden.shape[0] * n // 2
+    blocks = span // SHIFT
+    first_tok = lax.axis_index("wide") // (n // 2) * span
+    shifted = lax.dynamic_slice_in_dim(shift_heads, lax.axis_index("narrow") * heads_here, heads_here) > 0
+
+    doubled = jnp.concatenate([seg_ids[-SHIFT:], seg_ids], 0)
+    seg_here = lax.dynamic_slice_in_dim(doubled, first_tok, span + SHIFT)
+    seg_q = seg_here[SHIFT:, None]
+    windows = jnp.stack([seg_here[b * SHIFT : (b + 2) * SHIFT] for b in range(blocks)])
+    odd = (jnp.arange(blocks) % 2 == 1)[None, :, None]
+    reaches = (shifted[:, None, None] != odd) | (jnp.arange(2 * SHIFT) >= SHIFT)[None, None, :]
+    seg_k = jnp.where(reaches, windows[None], -1)[:, :, None, :]
+    return hub_layer(hidden, w_qkv.transpose(1, 0, 2), w_out, seg_q, seg_k)
+
+
 def solution(mesh):
     placed = (
         P(("groups", "wide"), None),
@@ -435,8 +1021,10 @@
         P("groups"),
         P(),
     )
+    shape = mesh.shape
+    hub = shape["groups"] == 2 and shape["wide"] == 4 and shape["narrow"] == 4
     return jax.shard_map(
-        per_device,
+        hub_per_device if hub else per_device,
         mesh=mesh,
         in_specs=placed,
         out_specs=P(("groups", "wide", "narrow"), None),

time: 190 us -> 156 us (0.82)
  Pallas kernels: 181 us -> 149 us
    pallas_call x1, Pallas kernels: 181 us -> 149 us  [hub_layer(): pl.pallas_call(functools.partial(hub_kernel, chunks, wo_chunks, direct),...]
where the time goes in v1:
time: 156 us; the launch traced here: 155 us
  Pallas kernels  149 us (96%)
  local copies, waits for them, and re-layouts  4.01 us (3%)
  other arithmetic  2.31 us (1%)
    pallas_call x1, Pallas kernels, hub_layer(): pl.pallas_call(functools.partial(hub_kernel, chunks, wo_chunks, direct),...  149 us

profile of v1, /device:TPU:1, one launch (start us, length us, event | category | flops | bytes accessed | tf_op | source)
XLA Modules:
  0.0 155.0 jit_solution(1138110113202515521)
XLA Ops:
  0.0 0.7 fusion.1
  0.7 0.1 broadcast_compare_fusion
  0.8 0.7 slice.18
  1.5 0.8 fusion
  2.3 0.7 or_select_fusion.segk_ref
  3.0 1.0 copy.6.segq_ref
  4.0 148.6 %shard_map.55 = bf16[128,4096]{1,0:T(8,128)(2,1)} custom-call(bf16[512,4096]{1,0:T(8,128)(2,1)} %hidden_ref.1, bf16[3,1024,512]{2,1,0:T(8,128)(2,1)} %bitcast.6, bf16[2048,1024]{1,0:T(8,128)(2,1)} %wo_ref.1, s32[1024,1]{1,0:T(8,128)} %copy.6.segq_ref, s32[4,4,1,512]{3,2,1,0:T(1,128)} %or_select_fusion.segk_ref), custom_call_target="tpu_custom_call" | custom-call | tf_op jit(solution)/shard_map/pallas_call | solution.py:967
  152.7 2.3 %copy.8 = bf16[128,4096]{1,0:T(8,128)(2,1)} copy(bf16[128,4096]{1,0:T(8,128)(2,1)} %shard_map.55) | data formatting | bytes 2097152
  (4 shorter events, 0.0 us)

commit v2 on v0

--- a/solution.py
+++ b/solution.py
@@ -16,6 +16,8 @@
 MESH = pl.DeviceIdType.MESH
 ROWS = 128
 WO_CHUNKS = 4
+HUB_ROWS = 256
+DIRECT = 1
 
 
 def layer_kernel(
@@ -427,6 +429,629 @@
     return layer(hidden, wq, wo, seg_q, seg_k)
 
 
+def hub_kernel(
+    row_chunks, direct,
+    hidden_ref, wq_ref, wo_ref, seg_ref, shift_ref, out_ref,
+    wbuf, hid, acc, q_buf, kv_buf, att, wo_buf, stage, seg_col,
+    own_sem, he_s, he_r, hx_s, hx_r, hc_s, hc_r,
+    wm_s, wm_r, we_s, we_r, wy_s, wy_r, kv_sem,
+    om_s, om_r, oe_s, oe_r, oy_s, oy_r,
+    ax_s, ax_r, ac_s, ac_r, res_s, res_r,
+):
+    n, narrow = lax.axis_size("wide"), lax.axis_size("narrow")
+    me = lax.axis_index("wide")
+    y = lax.axis_index("groups")
+    spot = lax.axis_index("narrow")
+    opp = 1 - y
+    side = me // (n // 2)
+    inner, outer = n // 2 - 1 + side, side * (n - 1)
+    far_inner, far_outer = n - 1 - inner, n - 1 - outer
+    is_inner, is_outer = me == inner, me == outer
+    high, low = spot // 2, lax.rem(spot, 2)
+    core_n, x_n = high * 2 + 1 - low, (1 - high) * 2 + low
+    diag_n = (1 - high) * 2 + 1 - low
+    depth = wq_ref.shape[1]
+    tok = hidden_ref.shape[0]
+    heads = wbuf.shape[0]
+    chunks = 2 * row_chunks
+    rows = depth // row_chunks
+    wo_chunks = 4
+    quarter = tok // narrow
+    span = 2 * tok
+    blocks = span // SHIFT
+    own_pos = 1 - side
+    own_row = pl.multiple_of(own_pos * tok, tok)
+    far_row = pl.multiple_of(side * tok, tok)
+    wo_half, wo_cols = wo_buf.shape[2], wo_buf.shape[3]
+    wo_rows, wo_lanes = wo_half // 2, wo_cols // 2
+    cols = wo_ref.shape[1]
+    to_core, to_x, to_y = {"narrow": core_n}, {"narrow": x_n}, {"groups": opp}
+    to_far, to_inner = {"wide": far_inner}, {"wide": inner}
+
+    def remote(src, dst, send, recv, device):
+        return pltpu.make_async_remote_copy(
+            src_ref=src, dst_ref=dst, send_sem=send, recv_sem=recv,
+            device_id=device, device_id_type=MESH,
+        )
+
+    def w_at(shard, part, c):
+        start = pl.multiple_of(shard * depth + lax.rem(c, row_chunks) * rows, rows)
+        return wbuf.at[c // row_chunks * 2 + part, :, pl.ds(start, rows)]
+
+    def wq_at(part, c):
+        start = pl.multiple_of(lax.rem(c, row_chunks) * rows, rows)
+        lane = pl.multiple_of((c // row_chunks * 2 + part) * HEAD_DIM, HEAD_DIM)
+        return wq_ref.at[:, pl.ds(start, rows), pl.ds(lane, HEAD_DIM)]
+
+    def o_at(shard, part, c):
+        start = pl.multiple_of(lax.rem(c, 2) * wo_rows, wo_rows)
+        return wo_buf.at[shard, part, pl.ds(start, wo_rows), pl.ds(pl.multiple_of(c // 2 * wo_lanes, wo_lanes), wo_lanes)]
+
+    def wo_at(part, c):
+        start = pl.multiple_of(part * wo_half + lax.rem(c, 2) * wo_rows, wo_rows)
+        lane = pl.multiple_of(spot * wo_cols + c // 2 * wo_lanes, wo_lanes)
+        return wo_ref.at[pl.ds(start, wo_rows), pl.ds(lane, wo_lanes)]
+
+    def h_at(row_n, k):
+        start = pl.multiple_of(far_row + row_n * quarter, quarter)
+        return hid.at[pl.ds(start, quarter), pl.ds(pl.multiple_of(k * depth, depth), depth)]
+
+    def h_end(k):
+        src = hidden_ref.at[
+            pl.ds(pl.multiple_of(spot * quarter, quarter), quarter), pl.ds(pl.multiple_of(k * depth, depth), depth)
+        ]
+        return remote(src, h_at(spot, k), he_s.at[k], he_r.at[k], to_inner)
+
+    def h_x(k, row_n):
+        return remote(h_at(row_n, k), h_at(row_n, k), hx_s.at[k], hx_r.at[k], to_x)
+
+    def h_core(j, k, row_n):
+        return remote(h_at(row_n, k), h_at(row_n, k), hc_s.at[j, k], hc_r.at[j, k], to_core)
+
+    def w_end(j, c):
+        part = y if j == 0 else opp
+        return remote(wq_at(part, c), w_at(outer, part, c), we_s.at[j, c], we_r.at[j, c], to_inner)
+
+    def w_mid_send(s, c):
+        if s == 0:
+            return remote(wq_at(y, c), w_at(inner, y, c), wm_s.at[s, c], wm_r.at[s, c], to_far)
+        return remote(w_at(outer, y, c), w_at(outer, y, c), wm_s.at[s, c], wm_r.at[s, c], to_far)
+
+    def far_shard(s):
+        return jnp.where(s == 0, far_inner, far_outer)
+
+    def w_mid_recv(s, c):
+        ref = w_at(far_shard(s), y, c)
+        return remote(ref, ref, wm_s.at[s, c], wm_r.at[s, c], to_far)
+
+    def y_shard(s):
+        return jnp.where(s == 2, outer, far_shard(s))
+
+    def w_y(s, c, part):
+        ref = w_at(y_shard(s), part, c)
+        return remote(ref, ref, wy_s.at[s, c], wy_r.at[s, c], to_y)
+
+    def o_end(j, c):
+        part = y if j == 0 else opp
+        return remote(wo_at(part, c), o_at(outer, part, c), oe_s.at[j, c], oe_r.at[j, c], to_inner)
+
+    def o_mid_send(s, c):
+        if s == 0:
+            return remote(wo_at(y, c), o_at(inner, y, c), om_s.at[s, c], om_r.at[s, c], to_far)
+        return remote(o_at(outer, y, c), o_at(outer, y, c), om_s.at[s, c], om_r.at[s, c], to_far)
+
+    def o_mid_recv(s, c):
+        ref = o_at(far_shard(s), y, c)
+        return remote(ref, ref, om_s.at[s, c], om_r.at[s, c], to_far)
+
+    def o_y(s, c, part):
+        ref = o_at(far_shard(s), part, c)
+        return remote(ref, ref, oy_s.at[s, c], oy_r.at[s, c], to_y)
+
+    def att_at(row_n, g, b):
+        return att.at[row_n, g, pl.ds(pl.multiple_of(b * SHIFT, SHIFT), SHIFT)]
+
+    def att_x(g, b, row_n):
+        ref = att_at(row_n, g, b)
+        return remote(ref, ref, ax_s.at[g, b], ax_r.at[g, b], to_x)
+
+    def att_core(j, g, b, row_n):
+        ref = att_at(row_n, g, b)
+        return remote(ref, ref, ac_s.at[j, g, b], ac_r.at[j, g, b], to_core)
+
+    shards = (inner, far_inner, outer, far_outer)
+    slots = ((0, 0, wo_cols), (1, 0, wo_cols), (2, 0, wo_cols), (3, 0, wo_lanes), (3, wo_lanes, wo_lanes))
+
+    def res_cols(slot, row_n):
+        order, lane, size = slots[slot]
+        return pl.ds(pl.multiple_of(shards[order] * cols + row_n * wo_cols + lane, size), size)
+
+    def result(slot, pos, to_n):
+        order, lane, size = slots[slot]
+        return remote(
+            stage.at[order, pl.ds(pl.multiple_of(pos * tok + to_n * quarter, quarter), quarter), lane : lane + size],
+            out_ref.at[:, res_cols(slot, spot)],
+            res_s.at[slot, pos, to_n], res_r.at[slot, spot],
+            {"wide": side * (n // 2) + pos, "narrow": to_n},
+        )
+
+    def result_arrival(slot, from_n):
+        ref = out_ref.at[:, res_cols(slot, from_n)]
+        return remote(ref, ref, res_s.at[slot, 0, 0], res_r.at[slot, from_n], to_core)
+
+    def kv_copy(g):
+        return remote(
+            kv_buf.at[pl.ds(2 * g, 2), :, pl.ds(span, SHIFT)], kv_buf.at[pl.ds(2 * g, 2), :, pl.ds(0, SHIFT)],
+            kv_sem.at[0, g], kv_sem.at[1, g], to_far,
+        )
+
+    barrier = pltpu.get_barrier_semaphore()
+
+    @pl.when(is_outer)
+    def _():
+        for p in range(narrow):
+            pl.semaphore_signal(barrier, inc=1, device_id={"wide": inner, "narrow": p}, device_id_type=MESH)
+        pl.semaphore_wait(barrier, narrow)
+
+        @pl.loop(0, n)
+        def _(k):
+            h_end(k).start()
+
+        def each_end(act):
+            @pl.loop(0, row_chunks)
+            def _(c):
+                act(w_end(0, c))
+
+            @pl.loop(0, direct)
+            def _(c):
+                act(w_end(1, c))
+
+            @pl.loop(row_chunks, chunks)
+            def _(c):
+                act(w_end(0, c))
+
+            @pl.loop(row_chunks, chunks)
+            def _(c):
+                act(w_end(1, c))
+
+            for j in range(2):
+                @pl.loop(0, wo_chunks)
+                def _(c):
+                    act(o_end(j, c))
+
+        each_end(lambda copy: copy.start())
+
+        @pl.loop(0, n)
+        def _(k):
+            h_end(k).wait_send()
+
+        each_end(lambda copy: copy.wait_send())
+        for slot in range(len(slots)):
+            for p in range(narrow):
+                result_arrival(slot, p).wait_recv()
+
+    @pl.when(is_inner)
+    def _():
+        own = [
+            pltpu.make_async_copy(
+                wq_ref.at[:, :, pl.ds(h * HEAD_DIM, HEAD_DIM)],
+                wbuf.at[h, :, pl.ds(pl.multiple_of(inner * depth, depth), depth)],
+                own_sem.at[h],
+            )
+            for h in range(heads)
+        ]
+        own.append(pltpu.make_async_copy(hidden_ref, hid.at[pl.ds(own_row, tok)], own_sem.at[heads]))
+        own += [
+            pltpu.make_async_copy(
+                wo_ref.at[pl.ds(h * wo_half, wo_half), pl.ds(pl.multiple_of(spot * wo_cols, wo_cols), wo_cols)],
+                wo_buf.at[inner, h],
+                own_sem.at[heads + 1 + h],
+            )
+            for h in range(2)
+        ]
+        for copy in own:
+            copy.start()
+        peers = [{"narrow": core_n}, {"narrow": x_n}, {"narrow": diag_n}, to_y, to_far]
+        peers += [{"wide": outer, "narrow": p} for p in range(narrow)]
+        for device in peers:
+            pl.semaphore_signal(barrier, inc=1, device_id=device, device_id_type=MESH)
+        pl.semaphore_wait(barrier, len(peers))
+
+        @pl.loop(0, chunks)
+        def _(c):
+            w_mid_send(0, c).start()
+
+        acc[...] = jnp.zeros_like(acc)
+        seg_rows = seg_ref.shape[0]
+        lanes = seg_ref.shape[1]
+        seg_first = side * (span // lanes)
+        for k in range(span // lanes):
+            line = seg_ref[pl.ds(seg_first + k, 1), :]
+            seg_col[k * lanes : (k + 1) * lanes, :] = jnp.broadcast_to(line, (lanes, lanes)).T
+
+        def add(row, size, shard, part, c):
+            start = pl.multiple_of(shard * depth + lax.rem(c, row_chunks) * rows, rows)
+            head = c // row_chunks * 2 + part
+            here = pl.ds(row, size)
+            piece = hid[here, pl.ds(start, rows)]
+            both = jnp.concatenate([wbuf[head, i, pl.ds(start, rows)] for i in range(2)], axis=1)
+            found = jnp.dot(piece, both, preferred_element_type=jnp.float32)
+            acc[head, 0, here] += found[:, :HEAD_DIM]
+            acc[head, 1, here] += found[:, HEAD_DIM:]
+            acc[head, 2, here] += jnp.dot(piece, wbuf[head, 2, pl.ds(start, rows)], preferred_element_type=jnp.float32)
+
+        def add_all(shard, part, c):
+            add(0, span, shard, part, c)
+
+        def add_at(t, shard, part, c):
+            @pl.when(t < chunks)
+            def _():
+                add(own_row, tok, shard, part, c)
+
+            @pl.when(t >= chunks)
+            def _():
+                add_all(shard, part, c)
+
+        for copy in own[: heads + 1]:
+            copy.wait()
+
+        @pl.loop(0, 2 * chunks)
+        def _(u):
+            add(own_row, tok, inner, u // chunks, lax.rem(u, chunks))
+
+        lag = row_chunks
+        lead = chunks - 2
+        catch_up = 4 * chunks - lag
+
+        @pl.loop(0, 2 * chunks)
+        def _(t):
+            s, c = t // chunks, lax.rem(t, chunks)
+            w_mid_recv(s, c).wait_recv()
+            w_y(s, c, y).start()
+
+            early = jnp.logical_and(t >= lead, t < lead + row_chunks)
+            later = jnp.logical_and(t >= lead + row_chunks + direct, t < lead + chunks + direct)
+            q = jnp.where(t < lead + row_chunks, t - lead, t - lead - direct)
+
+            @pl.when(jnp.logical_or(early, later))
+            def _():
+                w_end(0, q).wait_recv()
+                w_mid_send(1, q).start()
+
+            @pl.when(jnp.logical_and(early, q >= direct))
+            def _():
+                w_y(2, q, y).start()
+
+            @pl.when(jnp.logical_and(t >= 1, t < 1 + n))
+            def _():
+                h_end(t - 1).wait_recv()
+                h_x(t - 1, spot).start()
+                h_core(0, t - 1, spot).start()
+
+            @pl.when(jnp.logical_and(t >= 4, t < 4 + n))
+            def _():
+                h_x(t - 4, x_n).wait_recv()
+                h_core(1, t - 4, x_n).start()
+
+            @pl.when(t == chunks)
+            def _():
+                @pl.loop(0, n)
+                def _(k):
+                    h_core(0, k, core_n).wait_recv()
+                    h_core(1, k, diag_n).wait_recv()
+
+            add_at(t, far_shard(s), y, c)
+
+            @pl.when(t >= lag)
+            def _():
+                v = t - lag
+                w_y(v // chunks, lax.rem(v, chunks), opp).wait_recv()
+                add_at(t, far_shard(v // chunks), opp, lax.rem(v, chunks))
+
+            @pl.when(t >= chunks)
+            def _():
+                add_all(outer, y, t - chunks)
+                u0 = 4 * (t - chunks)
+
+                @pl.loop(u0, jnp.minimum(u0 + 4, catch_up))
+                def _(u):
+                    first = u < 2 * chunks
+                    part = jnp.where(first, u // chunks, jnp.where(u < 3 * chunks, y, opp))
+                    add(far_row, tok, jnp.where(first, inner, far_inner), part, lax.rem(u, chunks))
+
+            @pl.when(t >= chunks + row_chunks)
+            def _():
+                k = t - chunks - row_chunks
+
+                @pl.when(k < direct)
+                def _():
+                    w_end(1, k).wait_recv()
+
+                @pl.when(k >= direct)
+                def _():
+                    w_y(2, k, opp).wait_recv()
+
+                add_all(outer, opp, k)
+
+        causal = lax.broadcasted_iota(jnp.int32, (SHIFT, 2 * SHIFT), 1) <= (
+            lax.broadcasted_iota(jnp.int32, (SHIFT, 2 * SHIFT), 0) + SHIFT
+        )
+        per_block = SHIFT // lanes
+
+        def seg_line(b):
+            at = [lax.rem(seg_first + b * per_block + k + seg_rows, seg_rows) for k in range(per_block)]
+            return jnp.concatenate([seg_ref[pl.ds(i, 1), :] for i in at], axis=1)
+
+        def attend(g, b):
+            mine, seen = slice(b * SHIFT, (b + 1) * SHIFT), slice(b * SHIFT, (b + 2) * SHIFT)
+            seg_q = jnp.concatenate([seg_col[mine, :]] * (2 * per_block), axis=1)
+            near, prior = seg_line(b), seg_line(b - 1)
+            for k in range(2):
+                h = 2 * g + k
+                reach = shift_ref[spot * heads + h]
+                if b % 2 == 1:
+                    reach = 1 - reach
+                seg_k = jnp.concatenate([prior * reach + (reach - 1), near], axis=1)
+                scores = lax.dot_general(
+                    q_buf[h, mine], kv_buf[h, 0, seen], (((1,), (1,)), ((), ())),
+                    preferred_element_type=jnp.float32,
+                ) * (1.0 / math.sqrt(HEAD_DIM))
+                allowed = causal & (seg_q == seg_k)
+                scores = jnp.where(allowed, scores, masked_out)
+                exponent = jnp.exp(scores - jnp.max(scores, axis=-1, keepdims=True))
+                weights = exponent / jnp.sum(exponent, axis=-1, keepdims=True)
+                att[spot, g, mine, k * HEAD_DIM : (k + 1) * HEAD_DIM] = jnp.dot(
+                    weights.astype(jnp.bfloat16), kv_buf[h, 1, seen], preferred_element_type=jnp.float32
+                ).astype(jnp.bfloat16)
+            att_x(g, b, spot).start()
+            att_core(0, g, b, spot).start()
+
+        def relay(g, b):
+            att_x(g, b, x_n).wait_recv()
+            att_core(1, g, b, x_n).start()
+
+        def gathered(b):
+            for g in range(2):
+                att_core(0, g, b, core_n).wait_recv()
+                att_core(1, g, b, diag_n).wait_recv()
+
+        def settle(g):
+            for h in (2 * g, 2 * g + 1):
+                for i in range(2):
+                    kv_buf[h, i, SHIFT:] = acc[h, 1 + i].astype(jnp.bfloat16)
+            kv_copy(g).start()
+            for h in (2 * g, 2 * g + 1):
+                q_buf[h] = acc[h, 0].astype(jnp.bfloat16)
+
+        def multiply(slot, b):
+            order, lane, size = slots[slot]
+            mine = pl.ds(pl.multiple_of(b * SHIFT, SHIFT), SHIFT)
+            a_cols = att.shape[3]
+            total = None
+            for p in range(narrow):
+                for g in range(2):
+                    start = (p % (narrow // 2) * 2 + g) * a_cols
+                    term = jnp.dot(
+                        att[p, g, mine],
+                        wo_buf[shards[order], p // (narrow // 2), start : start + a_cols, lane : lane + size],
+                        preferred_element_type=jnp.float32,
+                    )
+                    total = term if total is None else total + term
+            done = total.astype(jnp.bfloat16)
+            stage[order, mine, lane : lane + size] = done
+            pos = b // (blocks // 2)
+            for k in range(SHIFT // quarter):
+                to_n = lax.rem(b, blocks // 2) * (SHIFT // quarter) + k
+                here = jnp.logical_and(pos == own_pos, spot == to_n)
+
+                @pl.when(here)
+                def _():
+                    out_ref[:, res_cols(slot, spot)] = done[k * quarter : (k + 1) * quarter]
+
+                @pl.when(jnp.logical_not(here))
+                def _():
+                    result(slot, pos, to_n).start()
+
+        def multiply_these(slot, first, count):
+            @pl.loop(0, count)
+            def _(k):
+                multiply(slot, lax.rem(first + k, blocks))
+
+        def near_wo(c):
+            o_mid_recv(0, c).wait_recv()
+            o_y(0, c, y).start()
+
+        def far_wo(c):
+            o_mid_recv(1, c).wait_recv()
+            o_y(1, c, y).start()
+
+        def pass_wo(c):
+            o_end(0, c).wait_recv()
+            o_mid_send(1, c).start()
+
+        def last_y(c):
+            w_y(1, c, opp).wait_recv()
+            add_all(far_outer, opp, c)
+
+        def last_end(c):
+            w_end(1, c).wait_recv()
+            add_all(outer, opp, c)
+
+        settle(0)
+
+        @pl.loop(0, wo_chunks)
+        def _(c):
+            o_mid_send(0, c).start()
+
+        attend(0, 1)
+        last_y(row_chunks)
+        attend(0, 2)
+        last_y(row_chunks + 1)
+        attend(0, 3)
+
+        @pl.loop(row_chunks, chunks - 2)
+        def _(c):
+            last_end(c)
+
+        relay(0, 1)
+        relay(0, 2)
+        last_y(row_chunks + 2)
+        kv_copy(0).wait_recv()
+        attend(0, 0)
+        relay(0, 3)
+
+        @pl.loop(chunks - 2, chunks)
+        def _(c):
+            last_end(c)
+
+        near_wo(0)
+        near_wo(1)
+        last_y(row_chunks + 3)
+        relay(0, 0)
+        settle(1)
+        near_wo(2)
+        attend(1, 1)
+        near_wo(3)
+        pass_wo(0)
+        attend(1, 2)
+        pass_wo(1)
+        attend(1, 3)
+        pass_wo(2)
+        pass_wo(3)
+        for copy in own[heads + 1 :]:
+            copy.wait()
+        relay(1, 1)
+        gathered(1)
+        multiply(0, 1)
+        relay(1, 2)
+        gathered(2)
+        multiply(0, 2)
+        kv_copy(1).wait_recv()
+        attend(1, 0)
+        far_wo(0)
+        relay(1, 3)
+        gathered(3)
+        multiply(0, 3)
+        far_wo(1)
+
+        @pl.loop(0, wo_chunks)
+        def _(c):
+            o_y(0, c, opp).wait_recv()
+
+        multiply_these(1, 1, 3)
+        far_wo(2)
+        relay(1, 0)
+
+        @pl.loop(0, wo_chunks)
+        def _(c):
+            o_end(1, c).wait_recv()
+
+        multiply_these(2, 1, 3)
+        far_wo(3)
+        gathered(0)
+        for slot in range(3):
+            multiply(slot, 0)
+        for k in range(2):
+            for c in range(2 * k, 2 * k + 2):
+                o_y(1, c, opp).wait_recv()
+            multiply_these(3 + k, side * (blocks // 2), blocks)
+
+        for slot in range(len(slots)):
+            for p in range(narrow):
+                @pl.when(spot != p)
+                def _():
+                    result_arrival(slot, p).wait_recv()
+
+        @pl.loop(0, n)
+        def _(k):
+            h_x(k, spot).wait_send()
+            h_core(0, k, spot).wait_send()
+            h_core(1, k, x_n).wait_send()
+
+        @pl.loop(0, chunks)
+        def _(c):
+            for s in range(2):
+                w_mid_send(s, c).wait_send()
+                w_y(s, c, y).wait_send()
+
+        @pl.loop(direct, row_chunks)
+        def _(c):
+            w_y(2, c, y).wait_send()
+
+        @pl.loop(0, wo_chunks)
+        def _(c):
+            for s in range(2):
+                o_mid_send(s, c).wait_send()
+                o_y(s, c, y).wait_send()
+
+        for g in range(2):
+            kv_copy(g).wait_send()
+
+            @pl.loop(0, blocks)
+            def _(b):
+                att_x(g, b, spot).wait_send()
+                att_core(0, g, b, spot).wait_send()
+                att_core(1, g, b, x_n).wait_send()
+
+        for slot in range(len(slots)):
+            for pos in range(2):
+                for to_n in range(narrow):
+                    @pl.when(jnp.logical_not(jnp.logical_and(pos == own_pos, spot == to_n)))
+                    def _():
+                        result(slot, pos, to_n).wait_send()
+
+
+def hub_layer(hidden, wq, wo, seg, shift_heads):
+    n, narrow = lax.axis_size("wide"), lax.axis_size("narrow")
+    tok, width = hidden.shape
+    heads = wq.shape[2] // HEAD_DIM
+    row_chunks = wq.shape[1] // HUB_ROWS
+    chunks, wo_chunks = 2 * row_chunks, 4
+    cols = wo.shape[1]
+    wo_half, wo_cols = wo.shape[0] // 2, cols // narrow
+    quarter, span = tok // narrow, 2 * tok
+    blocks = span // SHIFT
+    vmem = pl.BlockSpec(memory_space=pltpu.VMEM)
+    smem = pl.BlockSpec(memory_space=pltpu.SMEM)
+    hbm = pl.BlockSpec(memory_space=pl.ANY)
+    dma = pltpu.SemaphoreType.DMA
+    bf16 = jnp.bfloat16
+    return pl.pallas_call(
+        functools.partial(hub_kernel, row_chunks, DIRECT),
+        out_shape=jax.ShapeDtypeStruct((quarter, n * cols), bf16),
+        in_specs=[hbm, hbm, hbm, vmem, smem],
+        out_specs=vmem,
+        scratch_shapes=[
+            pltpu.VMEM((heads, 3, width, HEAD_DIM), bf16),
+            pltpu.VMEM((span, width), bf16),
+            pltpu.VMEM((heads, 3, span, HEAD_DIM), jnp.float32),
+            pltpu.VMEM((heads, span, HEAD_DIM), bf16),
+            pltpu.VMEM((heads, 2, span + SHIFT, HEAD_DIM), bf16),
+            pltpu.VMEM((narrow, 2, span, 2 * HEAD_DIM), bf16),
+            pltpu.VMEM((n, 2, wo_half, wo_cols), bf16),
+            pltpu.VMEM((n, span, wo_cols), bf16),
+            pltpu.VMEM((span, seg.shape[1]), jnp.int32),
+            dma((heads + 3,)),
+        ]
+        + [dma((n,))] * 4
+        + [dma((2, n))] * 2
+        + [dma((2, chunks))] * 4
+        + [dma((3, chunks))] * 2
+        + [dma((2, 2))]
+        + [dma((2, wo_chunks))] * 6
+        + [dma((2, blocks))] * 2
+        + [dma((2, 2, blocks))] * 2
+        + [dma((5, 2, narrow)), dma((5, narrow))],
+        compiler_params=pltpu.CompilerParams(
+            collective_id=0, has_side_effects=True, vmem_limit_bytes=58 * 1024 * 1024
+        ),
+    )(hidden, wq, wo, seg, shift_heads)
+
+
+def hub_per_device(hidden, w_qkv, w_out, seg_ids, shift_heads):
+    return hub_layer(hidden, w_qkv.transpose(1, 0, 2), w_out, seg_ids.reshape(-1, 128), shift_heads)
+
+
 def solution(mesh):
     placed = (
         P(("groups", "wide"), None),
@@ -435,8 +1060,10 @@
         P("groups"),
         P(),
     )
+    shape = mesh.shape
+    hub = shape["groups"] == 2 and shape["wide"] == 4 and shape["narrow"] == 4
     return jax.shard_map(
-        per_device,
+        hub_per_device if hub else per_device,
         mesh=mesh,
         in_specs=placed,
         out_specs=P(("groups", "wide", "narrow"), None),

time: 190 us -> 138 us (0.73); the launches traced: 187 us -> 138 us
  Pallas kernels: 181 us -> 135 us
  other arithmetic: 2.29 us -> 0 us
    pallas_call x1, Pallas kernels: 181 us -> 135 us  [hub_layer(): pl.pallas_call(functools.partial(hub_kernel, row_chunks, DIRECT), out_sha...]
where the time goes in v2:
time: 138 us
  Pallas kernels  135 us (98%)
  local copies, waits for them, and re-layouts  2.29 us (2%)
    pallas_call x1, Pallas kernels, hub_layer(): pl.pallas_call(functools.partial(hub_kernel, row_chunks, DIRECT), out_sha...  135 us

profile of v2, /device:TPU:1, one launch (start us, length us, event | category | flops | bytes accessed | tf_op | source)
XLA Modules:
  0.0 137.7 jit_solution(3998233772762461899)
XLA Ops:
  0.0 135.4 %shard_map.55 = bf16[128,4096]{1,0:T(8,128)(2,1)} custom-call(bf16[512,4096]{1,0:T(8,128)(2,1)} %hidden_ref.1, bf16[3,1024,512]{2,1,0:T(8,128)(2,1)} %bitcast.2, bf16[2048,1024]{1,0:T(8,128)(2,1)} %wo_ref.1, s32[16,128]{1,0:T(8,128)} %bitcast.3, s32[16]{0:T(128)} %shift_ref.1), custom_call_target="tpu_custom_call" | custom-call | tf_op jit(solution)/shard_map/pallas_call | solution.py:1019
  135.5 2.3 %copy.7 = bf16[128,4096]{1,0:T(8,128)(2,1)} copy(bf16[128,4096]{1,0:T(8,128)(2,1)} %shard_map.55) | data formatting | bytes 2097152

commit v3 on v2

--- a/solution.py
+++ b/solution.py
@@ -17,7 +17,7 @@
 ROWS = 128
 WO_CHUNKS = 4
 HUB_ROWS = 256
-DIRECT = 1
+DIRECT = 2
 
 
 def layer_kernel(
@@ -435,8 +435,8 @@
     wbuf, hid, acc, q_buf, kv_buf, att, wo_buf, stage, seg_col,
     own_sem, he_s, he_r, hx_s, hx_r, hc_s, hc_r,
     wm_s, wm_r, we_s, we_r, wy_s, wy_r, kv_sem,
-    om_s, om_r, oe_s, oe_r, oy_s, oy_r,
-    ax_s, ax_r, ac_s, ac_r, res_s, res_r,
+    om_s, om_r, oe_s, oe_r, oy_s, oy_r, od_s, od_r,
+    ax_s, ax_r, ae_s, ae_r, ac_s, ac_r, res_s, res_r,
 ):
     n, narrow = lax.axis_size("wide"), lax.axis_size("narrow")
     me = lax.axis_index("wide")
@@ -466,7 +466,10 @@
     wo_rows, wo_lanes = wo_half // 2, wo_cols // 2
     cols = wo_ref.shape[1]
     to_core, to_x, to_y = {"narrow": core_n}, {"narrow": x_n}, {"groups": opp}
-    to_far, to_inner = {"wide": far_inner}, {"wide": inner}
+    to_far, to_inner, to_outer = {"wide": far_inner}, {"wide": inner}, {"wide": outer}
+    my_pos = jnp.where(is_inner, own_pos, side)
+    my_first = my_pos * (blocks // 2)
+    first_b, second_b = my_first + 1 - my_pos, my_first + my_pos
 
     def remote(src, dst, send, recv, device):
         return pltpu.make_async_remote_copy(
@@ -544,8 +547,18 @@
         ref = o_at(far_shard(s), y, c)
         return remote(ref, ref, om_s.at[s, c], om_r.at[s, c], to_far)
 
+    def o_down(s, c):
+        if s == 0:
+            return remote(wo_at(y, c), o_at(inner, y, c), od_s.at[s, c], od_r.at[s, c], to_outer)
+        ref = o_at(far_shard(s - 1), y, c)
+        return remote(ref, ref, od_s.at[s, c], od_r.at[s, c], to_outer)
+
+    def o_down_recv(s, c):
+        ref = o_at(inner if s == 0 else far_shard(s - 1), y, c)
+        return remote(ref, ref, od_s.at[s, c], od_r.at[s, c], to_outer)
+
     def o_y(s, c, part):
-        ref = o_at(far_shard(s), part, c)
+        ref = o_at(inner if s == 2 else far_shard(s), part, c)
         return remote(ref, ref, oy_s.at[s, c], oy_r.at[s, c], to_y)
 
     def att_at(row_n, g, b):
@@ -559,25 +572,96 @@
         ref = att_at(row_n, g, b)
         return remote(ref, ref, ac_s.at[j, g, b], ac_r.at[j, g, b], to_core)
 
-    shards = (inner, far_inner, outer, far_outer)
+    def att_end(g, b):
+        ref = att_at(spot, g, b)
+        return remote(ref, ref, ae_s.at[g, b], ae_r.at[g, b], to_outer)
+
+    def share(g, b):
+        att_x(g, b, spot).start()
+        att_core(0, g, b, spot).start()
+
+    def relay(g, b):
+        att_x(g, b, x_n).wait_recv()
+        att_core(1, g, b, x_n).start()
+
+    def gathered(b):
+        for g in range(2):
+            att_core(0, g, b, core_n).wait_recv()
+            att_core(1, g, b, diag_n).wait_recv()
+
+    shards = (me, jnp.where(is_inner, far_inner, inner), jnp.where(is_inner, outer, far_inner), far_outer)
     slots = ((0, 0, wo_cols), (1, 0, wo_cols), (2, 0, wo_cols), (3, 0, wo_lanes), (3, wo_lanes, wo_lanes))
 
     def res_cols(slot, row_n):
         order, lane, size = slots[slot]
         return pl.ds(pl.multiple_of(shards[order] * cols + row_n * wo_cols + lane, size), size)
 
-    def result(slot, pos, to_n):
+    def result(slot, to_n):
         order, lane, size = slots[slot]
         return remote(
-            stage.at[order, pl.ds(pl.multiple_of(pos * tok + to_n * quarter, quarter), quarter), lane : lane + size],
+            stage.at[order, pl.ds(pl.multiple_of(to_n * quarter, quarter), quarter), lane : lane + size],
             out_ref.at[:, res_cols(slot, spot)],
-            res_s.at[slot, pos, to_n], res_r.at[slot, spot],
-            {"wide": side * (n // 2) + pos, "narrow": to_n},
+            res_s.at[slot, to_n], res_r.at[slot, spot], {"narrow": to_n},
         )
 
     def result_arrival(slot, from_n):
         ref = out_ref.at[:, res_cols(slot, from_n)]
-        return remote(ref, ref, res_s.at[slot, 0, 0], res_r.at[slot, from_n], to_core)
+        return remote(ref, ref, res_s.at[slot, 0], res_r.at[slot, from_n], to_core)
+
+    def multiply(slot, b):
+        order, lane, size = slots[slot]
+        mine = pl.ds(pl.multiple_of(b * SHIFT, SHIFT), SHIFT)
+        local = b - my_first
+        a_cols = att.shape[3]
+        total = None
+        for p in range(narrow):
+            for g in range(2):
+                start = (p % (narrow // 2) * 2 + g) * a_cols
+                term = jnp.dot(
+                    att[p, g, mine],
+                    wo_buf[shards[order], p // (narrow // 2), start : start + a_cols, lane : lane + size],
+                    preferred_element_type=jnp.float32,
+                )
+                total = term if total is None else total + term
+        done = total.astype(jnp.bfloat16)
+        stage[order, pl.ds(pl.multiple_of(local * SHIFT, SHIFT), SHIFT), lane : lane + size] = done
+        for k in range(SHIFT // quarter):
+            to_n = local * (SHIFT // quarter) + k
+
+            @pl.when(spot == to_n)
+            def _():
+                out_ref[:, res_cols(slot, spot)] = done[k * quarter : (k + 1) * quarter]
+
+            @pl.when(spot != to_n)
+            def _():
+                result(slot, to_n).start()
+
+    def multiply_both(slot):
+        @pl.loop(0, 2)
+        def _(k):
+            multiply(slot, jnp.where(k == 0, first_b, second_b))
+
+    def finish_sends(y_slots):
+        for slot in range(len(slots)):
+            for p in range(narrow):
+                @pl.when(spot != p)
+                def _():
+                    result_arrival(slot, p).wait_recv()
+        for slot in range(len(slots)):
+            for p in range(narrow):
+                @pl.when(spot != p)
+                def _():
+                    result(slot, p).wait_send()
+        for g in range(2):
+            for b in (first_b, second_b):
+                att_x(g, b, spot).wait_send()
+                att_core(0, g, b, spot).wait_send()
+                att_core(1, g, b, x_n).wait_send()
+
+        @pl.loop(0, wo_chunks)
+        def _(c):
+            for s in y_slots:
+                o_y(s, c, y).wait_send()
 
     def kv_copy(g):
         return remote(
@@ -587,28 +671,36 @@
 
     barrier = pltpu.get_barrier_semaphore()
 
+    def greet(peers):
+        for device in peers:
+            pl.semaphore_signal(barrier, inc=1, device_id=device, device_id_type=MESH)
+        pl.semaphore_wait(barrier, len(peers))
+
+    beside = [{"narrow": core_n}, {"narrow": x_n}, {"narrow": diag_n}, to_y]
+
+    def own_wo(h):
+        return pltpu.make_async_copy(
+            wo_ref.at[pl.ds(h * wo_half, wo_half), pl.ds(pl.multiple_of(spot * wo_cols, wo_cols), wo_cols)],
+            wo_buf.at[me, h],
+            own_sem.at[heads + 1 + h],
+        )
+
     @pl.when(is_outer)
     def _():
-        for p in range(narrow):
-            pl.semaphore_signal(barrier, inc=1, device_id={"wide": inner, "narrow": p}, device_id_type=MESH)
-        pl.semaphore_wait(barrier, narrow)
+        greet(beside + [to_inner])
 
         @pl.loop(0, n)
         def _(k):
             h_end(k).start()
 
         def each_end(act):
-            @pl.loop(0, row_chunks)
+            @pl.loop(0, chunks)
             def _(c):
                 act(w_end(0, c))
 
             @pl.loop(0, direct)
             def _(c):
                 act(w_end(1, c))
-
-            @pl.loop(row_chunks, chunks)
-            def _(c):
-                act(w_end(0, c))
 
             @pl.loop(row_chunks, chunks)
             def _(c):
@@ -620,15 +712,60 @@
                     act(o_end(j, c))
 
         each_end(lambda copy: copy.start())
+        for h in range(2):
+            own_wo(h).start()
+
+        def down(s, first, last):
+            @pl.loop(first, last)
+            def _(c):
+                o_down_recv(s, c).wait_recv()
+                o_y(2 if s == 0 else s - 1, c, y).start()
+
+        def take(g, b):
+            att_end(g, b).wait_recv()
+            share(g, b)
+
+        def y_arrived(s, first, last):
+            @pl.loop(first, last)
+            def _(c):
+                o_y(s, c, opp).wait_recv()
+
+        down(0, 0, wo_chunks)
+        for h in range(2):
+            own_wo(h).wait()
+        y_arrived(2, 0, wo_chunks)
+        take(0, first_b)
+        relay(0, first_b)
+        take(0, second_b)
+        down(1, 0, 2)
+        take(1, first_b)
+        relay(0, second_b)
+        relay(1, first_b)
+        gathered(first_b)
+        multiply(0, first_b)
+        multiply(1, first_b)
+        down(1, 2, wo_chunks)
+        take(1, second_b)
+        relay(1, second_b)
+        gathered(second_b)
+        multiply(0, second_b)
+        multiply(1, second_b)
+        down(2, 0, 1)
+        y_arrived(0, 0, wo_chunks)
+        multiply(2, first_b)
+        down(2, 1, 2)
+        multiply(2, second_b)
+        down(2, 2, wo_chunks)
+        for k in range(2):
+            y_arrived(1, 2 * k, 2 * k + 2)
+            multiply_both(3 + k)
 
         @pl.loop(0, n)
         def _(k):
             h_end(k).wait_send()
 
         each_end(lambda copy: copy.wait_send())
-        for slot in range(len(slots)):
-            for p in range(narrow):
-                result_arrival(slot, p).wait_recv()
+        finish_sends((0, 1, 2))
 
     @pl.when(is_inner)
     def _():
@@ -641,25 +778,19 @@
             for h in range(heads)
         ]
         own.append(pltpu.make_async_copy(hidden_ref, hid.at[pl.ds(own_row, tok)], own_sem.at[heads]))
-        own += [
-            pltpu.make_async_copy(
-                wo_ref.at[pl.ds(h * wo_half, wo_half), pl.ds(pl.multiple_of(spot * wo_cols, wo_cols), wo_cols)],
-                wo_buf.at[inner, h],
-                own_sem.at[heads + 1 + h],
-            )
-            for h in range(2)
-        ]
         for copy in own:
             copy.start()
-        peers = [{"narrow": core_n}, {"narrow": x_n}, {"narrow": diag_n}, to_y, to_far]
-        peers += [{"wide": outer, "narrow": p} for p in range(narrow)]
-        for device in peers:
-            pl.semaphore_signal(barrier, inc=1, device_id=device, device_id_type=MESH)
-        pl.semaphore_wait(barrier, len(peers))
+        for h in range(2):
+            own_wo(h).start()
+        greet(beside + [to_far, to_outer])
 
         @pl.loop(0, chunks)
         def _(c):
             w_mid_send(0, c).start()
+
+        @pl.loop(0, wo_chunks)
+        def _(c):
+            o_down(0, c).start()
 
         acc[...] = jnp.zeros_like(acc)
         seg_rows = seg_ref.shape[0]
@@ -692,7 +823,7 @@
             def _():
                 add_all(shard, part, c)
 
-        for copy in own[: heads + 1]:
+        for copy in own:
             copy.wait()
 
         @pl.loop(0, 2 * chunks)
@@ -709,16 +840,14 @@
             w_mid_recv(s, c).wait_recv()
             w_y(s, c, y).start()
 
-            early = jnp.logical_and(t >= lead, t < lead + row_chunks)
-            later = jnp.logical_and(t >= lead + row_chunks + direct, t < lead + chunks + direct)
-            q = jnp.where(t < lead + row_chunks, t - lead, t - lead - direct)
-
-            @pl.when(jnp.logical_or(early, later))
+            q = t - lead
+
+            @pl.when(jnp.logical_and(q >= 0, q < chunks))
             def _():
                 w_end(0, q).wait_recv()
                 w_mid_send(1, q).start()
 
-            @pl.when(jnp.logical_and(early, q >= direct))
+            @pl.when(jnp.logical_and(q >= direct, q < row_chunks))
             def _():
                 w_y(2, q, y).start()
 
@@ -761,7 +890,7 @@
 
             @pl.when(t >= chunks + row_chunks)
             def _():
-                k = t - chunks - row_chunks
+                k = lax.rem(t - chunks - row_chunks + direct, row_chunks)
 
                 @pl.when(k < direct)
                 def _():
@@ -803,17 +932,15 @@
                 att[spot, g, mine, k * HEAD_DIM : (k + 1) * HEAD_DIM] = jnp.dot(
                     weights.astype(jnp.bfloat16), kv_buf[h, 1, seen], preferred_element_type=jnp.float32
                 ).astype(jnp.bfloat16)
-            att_x(g, b, spot).start()
-            att_core(0, g, b, spot).start()
-
-        def relay(g, b):
-            att_x(g, b, x_n).wait_recv()
-            att_core(1, g, b, x_n).start()
-
-        def gathered(b):
-            for g in range(2):
-                att_core(0, g, b, core_n).wait_recv()
-                att_core(1, g, b, diag_n).wait_recv()
+            pos = b // (blocks // 2)
+
+            @pl.when(pos == own_pos)
+            def _():
+                share(g, b)
+
+            @pl.when(pos != own_pos)
+            def _():
+                att_end(g, b).start()
 
         def settle(g):
             for h in (2 * g, 2 * g + 1):
@@ -823,47 +950,15 @@
             for h in (2 * g, 2 * g + 1):
                 q_buf[h] = acc[h, 0].astype(jnp.bfloat16)
 
-        def multiply(slot, b):
-            order, lane, size = slots[slot]
-            mine = pl.ds(pl.multiple_of(b * SHIFT, SHIFT), SHIFT)
-            a_cols = att.shape[3]
-            total = None
-            for p in range(narrow):
-                for g in range(2):
-                    start = (p % (narrow // 2) * 2 + g) * a_cols
-                    term = jnp.dot(
-                        att[p, g, mine],
-                        wo_buf[shards[order], p // (narrow // 2), start : start + a_cols, lane : lane + size],
-                        preferred_element_type=jnp.float32,
-                    )
-                    total = term if total is None else total + term
-            done = total.astype(jnp.bfloat16)
-            stage[order, mine, lane : lane + size] = done
-            pos = b // (blocks // 2)
-            for k in range(SHIFT // quarter):
-                to_n = lax.rem(b, blocks // 2) * (SHIFT // quarter) + k
-                here = jnp.logical_and(pos == own_pos, spot == to_n)
-
-                @pl.when(here)
-                def _():
-                    out_ref[:, res_cols(slot, spot)] = done[k * quarter : (k + 1) * quarter]
-
-                @pl.when(jnp.logical_not(here))
-                def _():
-                    result(slot, pos, to_n).start()
-
-        def multiply_these(slot, first, count):
-            @pl.loop(0, count)
-            def _(k):
-                multiply(slot, lax.rem(first + k, blocks))
-
         def near_wo(c):
             o_mid_recv(0, c).wait_recv()
             o_y(0, c, y).start()
+            o_down(1, c).start()
 
         def far_wo(c):
             o_mid_recv(1, c).wait_recv()
             o_y(1, c, y).start()
+            o_down(2, c).start()
 
         def pass_wo(c):
             o_end(0, c).wait_recv()
@@ -878,11 +973,8 @@
             add_all(outer, opp, c)
 
         settle(0)
-
-        @pl.loop(0, wo_chunks)
-        def _(c):
+        for c in range(2):
             o_mid_send(0, c).start()
-
         attend(0, 1)
         last_y(row_chunks)
         attend(0, 2)
@@ -893,74 +985,63 @@
         def _(c):
             last_end(c)
 
-        relay(0, 1)
-        relay(0, 2)
+        relay(0, first_b)
         last_y(row_chunks + 2)
         kv_copy(0).wait_recv()
         attend(0, 0)
-        relay(0, 3)
 
         @pl.loop(chunks - 2, chunks)
         def _(c):
             last_end(c)
 
+        last_y(row_chunks + 3)
+        settle(1)
+        for c in range(2, wo_chunks):
+            o_mid_send(0, c).start()
+        attend(1, 1)
         near_wo(0)
         near_wo(1)
-        last_y(row_chunks + 3)
-        relay(0, 0)
-        settle(1)
-        near_wo(2)
-        attend(1, 1)
-        near_wo(3)
+        attend(1, 2)
         pass_wo(0)
-        attend(1, 2)
         pass_wo(1)
         attend(1, 3)
+        relay(0, second_b)
         pass_wo(2)
-        pass_wo(3)
-        for copy in own[heads + 1 :]:
-            copy.wait()
-        relay(1, 1)
-        gathered(1)
-        multiply(0, 1)
-        relay(1, 2)
-        gathered(2)
-        multiply(0, 2)
+        for h in range(2):
+            own_wo(h).wait()
+        relay(1, first_b)
         kv_copy(1).wait_recv()
         attend(1, 0)
+        pass_wo(3)
+        gathered(first_b)
+        multiply(0, first_b)
+        near_wo(2)
+        near_wo(3)
+        relay(1, second_b)
+        gathered(second_b)
+        multiply(0, second_b)
         far_wo(0)
-        relay(1, 3)
-        gathered(3)
-        multiply(0, 3)
+
+        @pl.loop(0, wo_chunks)
+        def _(c):
+            o_y(0, c, opp).wait_recv()
+
+        multiply(1, first_b)
         far_wo(1)
+        multiply(1, second_b)
 
         @pl.loop(0, wo_chunks)
         def _(c):
-            o_y(0, c, opp).wait_recv()
-
-        multiply_these(1, 1, 3)
+            o_end(1, c).wait_recv()
+
+        multiply(2, first_b)
         far_wo(2)
-        relay(1, 0)
-
-        @pl.loop(0, wo_chunks)
-        def _(c):
-            o_end(1, c).wait_recv()
-
-        multiply_these(2, 1, 3)
+        multiply(2, second_b)
         far_wo(3)
-        gathered(0)
-        for slot in range(3):
-            multiply(slot, 0)
         for k in range(2):
             for c in range(2 * k, 2 * k + 2):
                 o_y(1, c, opp).wait_recv()
-            multiply_these(3 + k, side * (blocks // 2), blocks)
-
-        for slot in range(len(slots)):
-            for p in range(narrow):
-                @pl.when(spot != p)
-                def _():
-                    result_arrival(slot, p).wait_recv()
+            multiply_both(3 + k)
 
         @pl.loop(0, n)
         def _(k):
@@ -982,23 +1063,15 @@
         def _(c):
             for s in range(2):
                 o_mid_send(s, c).wait_send()
-                o_y(s, c, y).wait_send()
-
+            for s in range(3):
+                o_down(s, c).wait_send()
+
+        other_first = (1 - own_pos) * (blocks // 2)
         for g in range(2):
             kv_copy(g).wait_send()
-
-            @pl.loop(0, blocks)
-            def _(b):
-                att_x(g, b, spot).wait_send()
-                att_core(0, g, b, spot).wait_send()
-                att_core(1, g, b, x_n).wait_send()
-
-        for slot in range(len(slots)):
-            for pos in range(2):
-                for to_n in range(narrow):
-                    @pl.when(jnp.logical_not(jnp.logical_and(pos == own_pos, spot == to_n)))
-                    def _():
-                        result(slot, pos, to_n).wait_send()
+            for k in range(blocks // 2):
+                att_end(g, other_first + k).wait_send()
+        finish_sends((0, 1))
 
 
 def hub_layer(hidden, wq, wo, seg, shift_heads):
@@ -1029,7 +1102,7 @@
             pltpu.VMEM((heads, 2, span + SHIFT, HEAD_DIM), bf16),
             pltpu.VMEM((narrow, 2, span, 2 * HEAD_DIM), bf16),
             pltpu.VMEM((n, 2, wo_half, wo_cols), bf16),
-            pltpu.VMEM((n, span, wo_cols), bf16),
+            pltpu.VMEM((n, tok, wo_cols), bf16),
             pltpu.VMEM((span, seg.shape[1]), jnp.int32),
             dma((heads + 3,)),
         ]
@@ -1038,10 +1111,11 @@
         + [dma((2, chunks))] * 4
         + [dma((3, chunks))] * 2
         + [dma((2, 2))]
-        + [dma((2, wo_chunks))] * 6
-        + [dma((2, blocks))] * 2
+        + [dma((2, wo_chunks))] * 4
+        + [dma((3, wo_chunks))] * 4
+        + [dma((2, blocks))] * 4
         + [dma((2, 2, blocks))] * 2
-        + [dma((5, 2, narrow)), dma((5, narrow))],
+        + [dma((5, narrow))] * 2,
         compiler_params=pltpu.CompilerParams(
             collective_id=0, has_side_effects=True, vmem_limit_bytes=58 * 1024 * 1024
         ),

time: 138 us -> 144 us (1.043)
  Pallas kernels: 135 us -> 141 us
    pallas_call x1, Pallas kernels: 135 us -> 141 us  [hub_layer(): pl.pallas_call(functools.partial(hub_kernel, row_chunks, DIRECT), out_sha...]
where the time goes in v3:
time: 144 us; the launch traced here: 143 us
  Pallas kernels  141 us (98%)
  local copies, waits for them, and re-layouts  2.29 us (2%)
    pallas_call x1, Pallas kernels, hub_layer(): pl.pallas_call(functools.partial(hub_kernel, row_chunks, DIRECT), out_sha...  141 us

profile of v3, /device:TPU:1, one launch (start us, length us, event | category | flops | bytes accessed | tf_op | source)
XLA Modules:
  0.0 143.3 jit_solution(3915587543565499560)
XLA Ops:
  0.0 141.0 %shard_map.55 = bf16[128,4096]{1,0:T(8,128)(2,1)} custom-call(bf16[512,4096]{1,0:T(8,128)(2,1)} %hidden_ref.1, bf16[3,1024,512]{2,1,0:T(8,128)(2,1)} %bitcast.2, bf16[2048,1024]{1,0:T(8,128)(2,1)} %wo_ref.1, s32[16,128]{1,0:T(8,128)} %bitcast.3, s32[16]{0:T(128)} %shift_ref.1), custom_call_target="tpu_custom_call" | custom-call | tf_op jit(solution)/shard_map/pallas_call | solution.py:1092
  141.0 2.3 %copy.7 = bf16[128,4096]{1,0:T(8,128)(2,1)} copy(bf16[128,4096]{1,0:T(8,128)(2,1)} %shard_map.55) | data formatting | bytes 2097152

commit v4 on v2

--- a/solution.py
+++ b/solution.py
@@ -17,7 +17,7 @@
 ROWS = 128
 WO_CHUNKS = 4
 HUB_ROWS = 256
-DIRECT = 1
+DIRECT = 2
 
 
 def layer_kernel(
@@ -560,7 +560,7 @@
         return remote(ref, ref, ac_s.at[j, g, b], ac_r.at[j, g, b], to_core)
 
     shards = (inner, far_inner, outer, far_outer)
-    slots = ((0, 0, wo_cols), (1, 0, wo_cols), (2, 0, wo_cols), (3, 0, wo_lanes), (3, wo_lanes, wo_lanes))
+    slots = ((0, 0, wo_cols), (1, 0, wo_cols)) + tuple((s, k * wo_lanes, wo_lanes) for s in (2, 3) for k in range(2))
 
     def res_cols(slot, row_n):
         order, lane, size = slots[slot]
@@ -598,7 +598,7 @@
             h_end(k).start()
 
         def each_end(act):
-            @pl.loop(0, row_chunks)
+            @pl.loop(0, chunks)
             def _(c):
                 act(w_end(0, c))
 
@@ -608,16 +608,12 @@
 
             @pl.loop(row_chunks, chunks)
             def _(c):
-                act(w_end(0, c))
-
-            @pl.loop(row_chunks, chunks)
-            def _(c):
                 act(w_end(1, c))
 
-            for j in range(2):
-                @pl.loop(0, wo_chunks)
-                def _(c):
-                    act(o_end(j, c))
+            for lane_half in range(2):
+                for j in range(2):
+                    for c in range(2 * lane_half, 2 * lane_half + 2):
+                        act(o_end(j, c))
 
         each_end(lambda copy: copy.start())
 
@@ -706,21 +702,19 @@
         @pl.loop(0, 2 * chunks)
         def _(t):
             s, c = t // chunks, lax.rem(t, chunks)
+            q = t - lead
+
+            @pl.when(jnp.logical_and(q >= 0, q < chunks))
+            def _():
+                w_end(0, q).wait_recv()
+                w_mid_send(1, q).start()
+
+            @pl.when(jnp.logical_and(q >= direct, q < row_chunks))
+            def _():
+                w_y(2, q, y).start()
+
             w_mid_recv(s, c).wait_recv()
             w_y(s, c, y).start()
-
-            early = jnp.logical_and(t >= lead, t < lead + row_chunks)
-            later = jnp.logical_and(t >= lead + row_chunks + direct, t < lead + chunks + direct)
-            q = jnp.where(t < lead + row_chunks, t - lead, t - lead - direct)
-
-            @pl.when(jnp.logical_or(early, later))
-            def _():
-                w_end(0, q).wait_recv()
-                w_mid_send(1, q).start()
-
-            @pl.when(jnp.logical_and(early, q >= direct))
-            def _():
-                w_y(2, q, y).start()
 
             @pl.when(jnp.logical_and(t >= 1, t < 1 + n))
             def _():
@@ -755,13 +749,15 @@
 
                 @pl.loop(u0, jnp.minimum(u0 + 4, catch_up))
                 def _(u):
-                    first = u < 2 * chunks
-                    part = jnp.where(first, u // chunks, jnp.where(u < 3 * chunks, y, opp))
-                    add(far_row, tok, jnp.where(first, inner, far_inner), part, lax.rem(u, chunks))
+                    turn = u // row_chunks
+                    near = lax.rem(turn, 4) < 2
+                    part = jnp.where(near, lax.rem(turn, 2), jnp.where(lax.rem(turn, 2) == 0, y, opp))
+                    c = lax.rem(u, row_chunks) + turn // 4 * row_chunks
+                    add(far_row, tok, jnp.where(near, inner, far_inner), part, c)
 
             @pl.when(t >= chunks + row_chunks)
             def _():
-                k = t - chunks - row_chunks
+                k = lax.rem(t - chunks - row_chunks + direct, row_chunks)
 
                 @pl.when(k < direct)
                 def _():
@@ -878,11 +874,8 @@
             add_all(outer, opp, c)
 
         settle(0)
-
-        @pl.loop(0, wo_chunks)
-        def _(c):
+        for c in range(3):
             o_mid_send(0, c).start()
-
         attend(0, 1)
         last_y(row_chunks)
         attend(0, 2)
@@ -894,67 +887,70 @@
             last_end(c)
 
         relay(0, 1)
+        kv_copy(0).wait_recv()
+        attend(0, 0)
         relay(0, 2)
         last_y(row_chunks + 2)
-        kv_copy(0).wait_recv()
-        attend(0, 0)
+        last_end(chunks - 2)
         relay(0, 3)
-
-        @pl.loop(chunks - 2, chunks)
-        def _(c):
-            last_end(c)
-
+        last_end(chunks - 1)
+        last_y(row_chunks + 3)
+        settle(1)
+        o_mid_send(0, 3).start()
+        attend(1, 1)
+        relay(0, 0)
         near_wo(0)
         near_wo(1)
-        last_y(row_chunks + 3)
-        relay(0, 0)
-        settle(1)
+        attend(1, 2)
         near_wo(2)
-        attend(1, 1)
-        near_wo(3)
         pass_wo(0)
-        attend(1, 2)
+        attend(1, 3)
         pass_wo(1)
-        attend(1, 3)
-        pass_wo(2)
-        pass_wo(3)
-        for copy in own[heads + 1 :]:
-            copy.wait()
+        own[heads + 1].wait()
+        own[heads + 2].wait()
         relay(1, 1)
         gathered(1)
         multiply(0, 1)
+        kv_copy(1).wait_recv()
+        attend(1, 0)
         relay(1, 2)
         gathered(2)
         multiply(0, 2)
-        kv_copy(1).wait_recv()
-        attend(1, 0)
-        far_wo(0)
+        near_wo(3)
+        for j in range(2):
+            o_end(1, j).wait_recv()
+        multiply_these(2, 1, 2)
         relay(1, 3)
         gathered(3)
         multiply(0, 3)
-        far_wo(1)
+        multiply(2, 3)
+        pass_wo(2)
 
         @pl.loop(0, wo_chunks)
         def _(c):
             o_y(0, c, opp).wait_recv()
 
         multiply_these(1, 1, 3)
+        pass_wo(3)
+        far_wo(0)
+        relay(1, 0)
+        gathered(0)
+        multiply(0, 0)
+        far_wo(1)
+        multiply(1, 0)
+        multiply(2, 0)
         far_wo(2)
-        relay(1, 0)
-
-        @pl.loop(0, wo_chunks)
-        def _(c):
-            o_end(1, c).wait_recv()
-
-        multiply_these(2, 1, 3)
         far_wo(3)
-        gathered(0)
-        for slot in range(3):
-            multiply(slot, 0)
-        for k in range(2):
-            for c in range(2 * k, 2 * k + 2):
-                o_y(1, c, opp).wait_recv()
-            multiply_these(3 + k, side * (blocks // 2), blocks)
+        first = side * (blocks // 2)
+        for j in range(2):
+            o_y(1, j, opp).wait_recv()
+        multiply_these(4, first, blocks)
+        for j in range(2):
+            o_end(1, 2 + j).wait_recv()
+        multiply_these(3, first, blocks)
+        for j in range(2):
+            o_y(1, 2 + j, opp).wait_recv()
+        multiply_these(5, first, blocks)
 
         for slot in range(len(slots)):
             for p in range(narrow):
@@ -1018,7 +1014,7 @@
     bf16 = jnp.bfloat16
     return pl.pallas_call(
         functools.partial(hub_kernel, row_chunks, DIRECT),
-        out_shape=jax.ShapeDtypeStruct((quarter, n * cols), bf16),
+        out_shape=pltpu.VMEM((quarter, n * cols), bf16),
         in_specs=[hbm, hbm, hbm, vmem, smem],
         out_specs=vmem,
         scratch_shapes=[
@@ -1041,7 +1037,7 @@
         + [dma((2, wo_chunks))] * 6
         + [dma((2, blocks))] * 2
         + [dma((2, 2, blocks))] * 2
-        + [dma((5, 2, narrow)), dma((5, narrow))],
+        + [dma((6, 2, narrow)), dma((6, narrow))],
         compiler_params=pltpu.CompilerParams(
             collective_id=0, has_side_effects=True, vmem_limit_bytes=58 * 1024 * 1024
         ),

time: 138 us -> 131 us (0.949)
  Pallas kernels: 135 us -> 129 us
    pallas_call x1, Pallas kernels: 135 us -> 129 us  [hub_layer(): pl.pallas_call(functools.partial(hub_kernel, row_chunks, DIRECT), out_sha...]
where the time goes in v4:
time: 131 us; the launch traced here: 130 us
  Pallas kernels  129 us (98%)
    pallas_call x1, Pallas kernels, hub_layer(): pl.pallas_call(functools.partial(hub_kernel, row_chunks, DIRECT), out_sha...  129 us

profile of v4, /device:TPU:1, one launch (start us, length us, event | category | flops | bytes accessed | tf_op | source)
XLA Modules:
  0.0 130.3 jit_solution(11418893376991404657)
XLA Ops:
  0.0 129.3 %shard_map.55 = bf16[128,4096]{1,0:T(8,128)(2,1)S(1)} custom-call(bf16[512,4096]{1,0:T(8,128)(2,1)} %hidden_ref.1, bf16[3,1024,512]{2,1,0:T(8,128)(2,1)} %bitcast.2, bf16[2048,1024]{1,0:T(8,128)(2,1)} %wo_ref.1, s32[16,128]{1,0:T(8,128)} %bitcast.3, s32[16]{0:T(128)} %shift_ref.1), custom_call_target="tpu_custom_call" | custom-call | tf_op jit(solution)/shard_map/pallas_call | solution.py:1015
  129.3 1.0 copy.7

commit v5 on v4

--- a/solution.py
+++ b/solution.py
@@ -433,10 +433,7 @@
     row_chunks, direct,
     hidden_ref, wq_ref, wo_ref, seg_ref, shift_ref, out_ref,
     wbuf, hid, acc, q_buf, kv_buf, att, wo_buf, stage, seg_col,
-    own_sem, he_s, he_r, hx_s, hx_r, hc_s, hc_r,
-    wm_s, wm_r, we_s, we_r, wy_s, wy_r, kv_sem,
-    om_s, om_r, oe_s, oe_r, oy_s, oy_r,
-    ax_s, ax_r, ac_s, ac_r, res_s, res_r,
+    own_sem, sends, joint, he_r, hx_r, wm_r, we_r, wy_r, w0_r, kv_r, om_r, oe_r, od_r, ax_r, ae_r,
 ):
     n, narrow = lax.axis_size("wide"), lax.axis_size("narrow")
     me = lax.axis_index("wide")
@@ -455,7 +452,8 @@
     heads = wbuf.shape[0]
     chunks = 2 * row_chunks
     rows = depth // row_chunks
-    wo_chunks = 4
+    wo_chunks = 8
+    sub = wo_chunks // 4
     quarter = tok // narrow
     span = 2 * tok
     blocks = span // SHIFT
@@ -463,10 +461,11 @@
     own_row = pl.multiple_of(own_pos * tok, tok)
     far_row = pl.multiple_of(side * tok, tok)
     wo_half, wo_cols = wo_buf.shape[2], wo_buf.shape[3]
-    wo_rows, wo_lanes = wo_half // 2, wo_cols // 2
+    wo_rows, wo_lanes = wo_half // (2 * sub), wo_cols // 2
     cols = wo_ref.shape[1]
     to_core, to_x, to_y = {"narrow": core_n}, {"narrow": x_n}, {"groups": opp}
-    to_far, to_inner = {"wide": far_inner}, {"wide": inner}
+    to_far, to_inner, to_outer = {"wide": far_inner}, {"wide": inner}, {"wide": outer}
+    my_pos = jnp.where(is_inner, own_pos, side)
 
     def remote(src, dst, send, recv, device):
         return pltpu.make_async_remote_copy(
@@ -474,6 +473,12 @@
             device_id=device, device_id_type=MESH,
         )
 
+    def arrived(place, ref):
+        remote(ref, ref, sends.at[0], joint.at[place], to_core).wait_recv()
+
+    def sent(place, ref):
+        remote(ref, ref, sends.at[place], joint.at[0], to_core).wait_send()
+
     def w_at(shard, part, c):
         start = pl.multiple_of(shard * depth + lax.rem(c, row_chunks) * rows, rows)
         return wbuf.at[c // row_chunks * 2 + part, :, pl.ds(start, rows)]
@@ -484,12 +489,13 @@
         return wq_ref.at[:, pl.ds(start, rows), pl.ds(lane, HEAD_DIM)]
 
     def o_at(shard, part, c):
-        start = pl.multiple_of(lax.rem(c, 2) * wo_rows, wo_rows)
-        return wo_buf.at[shard, part, pl.ds(start, wo_rows), pl.ds(pl.multiple_of(c // 2 * wo_lanes, wo_lanes), wo_lanes)]
+        start = pl.multiple_of(lax.rem(c, 2 * sub) * wo_rows, wo_rows)
+        lane = pl.multiple_of(c // (2 * sub) * wo_lanes, wo_lanes)
+        return wo_buf.at[shard, part, pl.ds(start, wo_rows), pl.ds(lane, wo_lanes)]
 
     def wo_at(part, c):
-        start = pl.multiple_of(part * wo_half + lax.rem(c, 2) * wo_rows, wo_rows)
-        lane = pl.multiple_of(spot * wo_cols + c // 2 * wo_lanes, wo_lanes)
+        start = pl.multiple_of(part * wo_half + lax.rem(c, 2 * sub) * wo_rows, wo_rows)
+        lane = pl.multiple_of(spot * wo_cols + c // (2 * sub) * wo_lanes, wo_lanes)
         return wo_ref.at[pl.ds(start, wo_rows), pl.ds(lane, wo_lanes)]
 
     def h_at(row_n, k):
@@ -500,67 +506,88 @@
         src = hidden_ref.at[
             pl.ds(pl.multiple_of(spot * quarter, quarter), quarter), pl.ds(pl.multiple_of(k * depth, depth), depth)
         ]
-        return remote(src, h_at(spot, k), he_s.at[k], he_r.at[k], to_inner)
+        return remote(src, h_at(spot, k), sends.at[0], he_r.at[k], to_inner)
 
     def h_x(k, row_n):
-        return remote(h_at(row_n, k), h_at(row_n, k), hx_s.at[k], hx_r.at[k], to_x)
-
-    def h_core(j, k, row_n):
-        return remote(h_at(row_n, k), h_at(row_n, k), hc_s.at[j, k], hc_r.at[j, k], to_core)
+        return remote(h_at(row_n, k), h_at(row_n, k), sends.at[0], hx_r.at[k], to_x)
+
+    def h_core(k, row_n):
+        return remote(h_at(row_n, k), h_at(row_n, k), sends.at[0], joint.at[0], to_core)
 
     def w_end(j, c):
         part = y if j == 0 else opp
-        return remote(wq_at(part, c), w_at(outer, part, c), we_s.at[j, c], we_r.at[j, c], to_inner)
+        return remote(wq_at(part, c), w_at(outer, part, c), sends.at[1], we_r.at[j, c], to_inner)
 
     def w_mid_send(s, c):
         if s == 0:
-            return remote(wq_at(y, c), w_at(inner, y, c), wm_s.at[s, c], wm_r.at[s, c], to_far)
-        return remote(w_at(outer, y, c), w_at(outer, y, c), wm_s.at[s, c], wm_r.at[s, c], to_far)
+            return remote(wq_at(y, c), w_at(inner, y, c), sends.at[1], wm_r.at[s, c], to_far)
+        return remote(w_at(outer, y, c), w_at(outer, y, c), sends.at[1], wm_r.at[s, c], to_far)
 
     def far_shard(s):
         return jnp.where(s == 0, far_inner, far_outer)
 
     def w_mid_recv(s, c):
         ref = w_at(far_shard(s), y, c)
-        return remote(ref, ref, wm_s.at[s, c], wm_r.at[s, c], to_far)
-
-    def y_shard(s):
-        return jnp.where(s == 2, outer, far_shard(s))
+        return remote(ref, ref, sends.at[1], wm_r.at[s, c], to_far)
 
     def w_y(s, c, part):
-        ref = w_at(y_shard(s), part, c)
-        return remote(ref, ref, wy_s.at[s, c], wy_r.at[s, c], to_y)
+        ref = w_at(far_shard(s), part, c)
+        return remote(ref, ref, sends.at[1], wy_r.at[s, c], to_y)
+
+    def w_y_outer(c, part):
+        ref = w_at(outer, part, c)
+        return remote(ref, ref, sends.at[2], w0_r.at[c], to_y)
 
     def o_end(j, c):
         part = y if j == 0 else opp
-        return remote(wo_at(part, c), o_at(outer, part, c), oe_s.at[j, c], oe_r.at[j, c], to_inner)
+        return remote(wo_at(part, c), o_at(outer, part, c), sends.at[4], oe_r.at[c] if j == 0 else joint.at[4 + c // (2 * sub)], to_inner)
 
     def o_mid_send(s, c):
         if s == 0:
-            return remote(wo_at(y, c), o_at(inner, y, c), om_s.at[s, c], om_r.at[s, c], to_far)
-        return remote(o_at(outer, y, c), o_at(outer, y, c), om_s.at[s, c], om_r.at[s, c], to_far)
+            return remote(wo_at(y, c), o_at(inner, y, c), sends.at[4], om_r.at[s, c], to_far)
+        return remote(o_at(outer, y, c), o_at(outer, y, c), sends.at[4], om_r.at[s, c], to_far)
 
     def o_mid_recv(s, c):
         ref = o_at(far_shard(s), y, c)
-        return remote(ref, ref, om_s.at[s, c], om_r.at[s, c], to_far)
+        return remote(ref, ref, sends.at[4], om_r.at[s, c], to_far)
+
+    def o_down(c):
+        return remote(wo_at(y, c), o_at(inner, y, c), sends.at[5], od_r.at[c], to_outer)
 
     def o_y(s, c, part):
-        ref = o_at(far_shard(s), part, c)
-        return remote(ref, ref, oy_s.at[s, c], oy_r.at[s, c], to_y)
+        ref = o_at(inner if s == 2 else far_shard(s), part, c)
+        place = (1, 2 + c // (2 * sub), 6)[s]
+        return remote(ref, ref, sends.at[5 if s == 2 else 4], joint.at[place], to_y)
 
     def att_at(row_n, g, b):
         return att.at[row_n, g, pl.ds(pl.multiple_of(b * SHIFT, SHIFT), SHIFT)]
 
     def att_x(g, b, row_n):
         ref = att_at(row_n, g, b)
-        return remote(ref, ref, ax_s.at[g, b], ax_r.at[g, b], to_x)
-
-    def att_core(j, g, b, row_n):
+        return remote(ref, ref, sends.at[6], ax_r.at[g, b], to_x)
+
+    def att_core(g, b, row_n):
         ref = att_at(row_n, g, b)
-        return remote(ref, ref, ac_s.at[j, g, b], ac_r.at[j, g, b], to_core)
+        return remote(ref, ref, sends.at[6], joint.at[8 + b], to_core)
+
+    def att_end(g, b):
+        ref = att_at(spot, g, b)
+        return remote(ref, ref, sends.at[7], ae_r.at[g, b], to_outer)
+
+    def share(g, b):
+        att_x(g, b, spot).start()
+        att_core(g, b, spot).start()
+
+    def relay(g, b):
+        att_x(g, b, x_n).wait_recv()
+        att_core(g, b, x_n).start()
+
+    def gathered(b):
+        arrived(8 + b, att.at[pl.ds(0, narrow // 2), :, pl.ds(pl.multiple_of(b * SHIFT, SHIFT), SHIFT)])
 
     shards = (inner, far_inner, outer, far_outer)
     slots = ((0, 0, wo_cols), (1, 0, wo_cols)) + tuple((s, k * wo_lanes, wo_lanes) for s in (2, 3) for k in range(2))
+    slots += ((2, 0, wo_cols),)
 
     def res_cols(slot, row_n):
         order, lane, size = slots[slot]
@@ -571,27 +598,64 @@
         return remote(
             stage.at[order, pl.ds(pl.multiple_of(pos * tok + to_n * quarter, quarter), quarter), lane : lane + size],
             out_ref.at[:, res_cols(slot, spot)],
-            res_s.at[slot, pos, to_n], res_r.at[slot, spot],
+            sends.at[8], joint.at[7],
             {"wide": side * (n // 2) + pos, "narrow": to_n},
         )
 
-    def result_arrival(slot, from_n):
-        ref = out_ref.at[:, res_cols(slot, from_n)]
-        return remote(ref, ref, res_s.at[slot, 0, 0], res_r.at[slot, from_n], to_core)
+    def multiply(slot, b):
+        order, lane, size = slots[slot]
+        mine = pl.ds(pl.multiple_of(b * SHIFT, SHIFT), SHIFT)
+        a_cols = att.shape[3]
+        total = None
+        for p in range(narrow):
+            for g in range(2):
+                start = (p % (narrow // 2) * 2 + g) * a_cols
+                term = jnp.dot(
+                    att[p, g, mine],
+                    wo_buf[shards[order], p // (narrow // 2), start : start + a_cols, lane : lane + size],
+                    preferred_element_type=jnp.float32,
+                )
+                total = term if total is None else total + term
+        done = total.astype(jnp.bfloat16)
+        stage[order, mine, lane : lane + size] = done
+        pos = b // (blocks // 2)
+        for k in range(SHIFT // quarter):
+            to_n = lax.rem(b, blocks // 2) * (SHIFT // quarter) + k
+            here = jnp.logical_and(pos == my_pos, spot == to_n)
+
+            @pl.when(here)
+            def _():
+                out_ref[:, res_cols(slot, spot)] = done[k * quarter : (k + 1) * quarter]
+
+            @pl.when(jnp.logical_not(here))
+            def _():
+                result(slot, pos, to_n).start()
 
     def kv_copy(g):
         return remote(
             kv_buf.at[pl.ds(2 * g, 2), :, pl.ds(span, SHIFT)], kv_buf.at[pl.ds(2 * g, 2), :, pl.ds(0, SHIFT)],
-            kv_sem.at[0, g], kv_sem.at[1, g], to_far,
+            sends.at[3], kv_r.at[g], to_far,
         )
 
     barrier = pltpu.get_barrier_semaphore()
+    beside = [{"narrow": core_n}, {"narrow": x_n}, {"narrow": diag_n}, to_y]
+
+    def greet(peers):
+        for device in peers:
+            pl.semaphore_signal(barrier, inc=1, device_id=device, device_id_type=MESH)
+        pl.semaphore_wait(barrier, len(peers))
+
+    def own_wo(h):
+        return pltpu.make_async_copy(
+            wo_ref.at[pl.ds(h * wo_half, wo_half), pl.ds(pl.multiple_of(spot * wo_cols, wo_cols), wo_cols)],
+            wo_buf.at[me, h],
+            own_sem.at[2 + h],
+        )
+
 
     @pl.when(is_outer)
     def _():
-        for p in range(narrow):
-            pl.semaphore_signal(barrier, inc=1, device_id={"wide": inner, "narrow": p}, device_id_type=MESH)
-        pl.semaphore_wait(barrier, narrow)
+        greet(beside + [{"wide": inner, "narrow": p} for p in range(narrow)])
 
         @pl.loop(0, n)
         def _(k):
@@ -612,19 +676,59 @@
 
             for lane_half in range(2):
                 for j in range(2):
-                    for c in range(2 * lane_half, 2 * lane_half + 2):
+                    @pl.loop(lane_half * 2 * sub, (lane_half + 1) * 2 * sub)
+                    def _(c):
                         act(o_end(j, c))
 
         each_end(lambda copy: copy.start())
-
-        @pl.loop(0, n)
-        def _(k):
-            h_end(k).wait_send()
-
-        each_end(lambda copy: copy.wait_send())
-        for slot in range(len(slots)):
-            for p in range(narrow):
-                result_arrival(slot, p).wait_recv()
+        for h in range(2):
+            own_wo(h).start()
+
+        @pl.loop(0, wo_chunks)
+        def _(c):
+            o_down(c).wait_recv()
+            o_y(2, c, y).start()
+
+        arrived(6, wo_buf.at[inner, opp])
+        for h in range(2):
+            own_wo(h).wait()
+
+        def take(g, b):
+            att_end(g, b).wait_recv()
+            share(g, b)
+
+        first_b, second_b = side + 1, 3 * side
+        take(0, first_b)
+        relay(0, first_b)
+        take(0, second_b)
+        relay(0, second_b)
+        take(1, first_b)
+
+        @pl.when(side == 1)
+        def _():
+            take(1, second_b)
+
+        relay(1, first_b)
+
+        @pl.when(side == 0)
+        def _():
+            take(1, second_b)
+
+        gathered(first_b)
+        multiply(0, first_b)
+        multiply(6, first_b)
+        relay(1, second_b)
+        gathered(second_b)
+        multiply(0, second_b)
+        multiply(6, second_b)
+
+        sent(0, hid.at[pl.ds(0, quarter)])
+        sent(1, wbuf.at[0, :, pl.ds(0, (chunks + direct + row_chunks) * rows)])
+        sent(4, wo_buf.at[0])
+        sent(5, wo_buf.at[0, 0])
+        sent(6, att.at[pl.ds(0, 3), 0])
+        sent(8, stage.at[0, pl.ds(0, 2 * (narrow - 1) * quarter)])
+        arrived(7, out_ref.at[:, pl.ds(0, (4 * narrow - 2) * wo_cols)])
 
     @pl.when(is_inner)
     def _():
@@ -632,30 +736,24 @@
             pltpu.make_async_copy(
                 wq_ref.at[:, :, pl.ds(h * HEAD_DIM, HEAD_DIM)],
                 wbuf.at[h, :, pl.ds(pl.multiple_of(inner * depth, depth), depth)],
-                own_sem.at[h],
+                own_sem.at[0],
             )
             for h in range(heads)
         ]
-        own.append(pltpu.make_async_copy(hidden_ref, hid.at[pl.ds(own_row, tok)], own_sem.at[heads]))
-        own += [
-            pltpu.make_async_copy(
-                wo_ref.at[pl.ds(h * wo_half, wo_half), pl.ds(pl.multiple_of(spot * wo_cols, wo_cols), wo_cols)],
-                wo_buf.at[inner, h],
-                own_sem.at[heads + 1 + h],
-            )
-            for h in range(2)
-        ]
+        own.append(pltpu.make_async_copy(hidden_ref, hid.at[pl.ds(own_row, tok)], own_sem.at[1]))
         for copy in own:
             copy.start()
-        peers = [{"narrow": core_n}, {"narrow": x_n}, {"narrow": diag_n}, to_y, to_far]
-        peers += [{"wide": outer, "narrow": p} for p in range(narrow)]
-        for device in peers:
-            pl.semaphore_signal(barrier, inc=1, device_id=device, device_id_type=MESH)
-        pl.semaphore_wait(barrier, len(peers))
+        for h in range(2):
+            own_wo(h).start()
+        greet(beside + [to_far] + [{"wide": outer, "narrow": p} for p in range(narrow)])
 
         @pl.loop(0, chunks)
         def _(c):
             w_mid_send(0, c).start()
+
+        @pl.loop(0, wo_chunks)
+        def _(c):
+            o_down(c).start()
 
         acc[...] = jnp.zeros_like(acc)
         seg_rows = seg_ref.shape[0]
@@ -688,8 +786,12 @@
             def _():
                 add_all(shard, part, c)
 
-        for copy in own[: heads + 1]:
-            copy.wait()
+        pltpu.make_async_copy(
+            wbuf.at[:, :, pl.ds(0, depth)],
+            wbuf.at[:, :, pl.ds(pl.multiple_of(inner * depth, depth), depth)],
+            own_sem.at[0],
+        ).wait()
+        own[heads].wait()
 
         @pl.loop(0, 2 * chunks)
         def _(u):
@@ -711,7 +813,7 @@
 
             @pl.when(jnp.logical_and(q >= direct, q < row_chunks))
             def _():
-                w_y(2, q, y).start()
+                w_y_outer(q, y).start()
 
             w_mid_recv(s, c).wait_recv()
             w_y(s, c, y).start()
@@ -720,19 +822,16 @@
             def _():
                 h_end(t - 1).wait_recv()
                 h_x(t - 1, spot).start()
-                h_core(0, t - 1, spot).start()
+                h_core(t - 1, spot).start()
 
             @pl.when(jnp.logical_and(t >= 4, t < 4 + n))
             def _():
                 h_x(t - 4, x_n).wait_recv()
-                h_core(1, t - 4, x_n).start()
+                h_core(t - 4, x_n).start()
 
             @pl.when(t == chunks)
             def _():
-                @pl.loop(0, n)
-                def _(k):
-                    h_core(0, k, core_n).wait_recv()
-                    h_core(1, k, diag_n).wait_recv()
+                arrived(0, hid.at[pl.ds(far_row, narrow // 2 * quarter)])
 
             add_at(t, far_shard(s), y, c)
 
@@ -765,7 +864,7 @@
 
                 @pl.when(k >= direct)
                 def _():
-                    w_y(2, k, opp).wait_recv()
+                    w_y_outer(k, opp).wait_recv()
 
                 add_all(outer, opp, k)
 
@@ -799,17 +898,11 @@
                 att[spot, g, mine, k * HEAD_DIM : (k + 1) * HEAD_DIM] = jnp.dot(
                     weights.astype(jnp.bfloat16), kv_buf[h, 1, seen], preferred_element_type=jnp.float32
                 ).astype(jnp.bfloat16)
-            att_x(g, b, spot).start()
-            att_core(0, g, b, spot).start()
-
-        def relay(g, b):
-            att_x(g, b, x_n).wait_recv()
-            att_core(1, g, b, x_n).start()
-
-        def gathered(b):
-            for g in range(2):
-                att_core(0, g, b, core_n).wait_recv()
-                att_core(1, g, b, diag_n).wait_recv()
+            share(g, b)
+
+            @pl.when(b // (blocks // 2) == side)
+            def _():
+                att_end(g, b).start()
 
         def settle(g):
             for h in (2 * g, 2 * g + 1):
@@ -819,51 +912,37 @@
             for h in (2 * g, 2 * g + 1):
                 q_buf[h] = acc[h, 0].astype(jnp.bfloat16)
 
-        def multiply(slot, b):
-            order, lane, size = slots[slot]
-            mine = pl.ds(pl.multiple_of(b * SHIFT, SHIFT), SHIFT)
-            a_cols = att.shape[3]
-            total = None
-            for p in range(narrow):
-                for g in range(2):
-                    start = (p % (narrow // 2) * 2 + g) * a_cols
-                    term = jnp.dot(
-                        att[p, g, mine],
-                        wo_buf[shards[order], p // (narrow // 2), start : start + a_cols, lane : lane + size],
-                        preferred_element_type=jnp.float32,
-                    )
-                    total = term if total is None else total + term
-            done = total.astype(jnp.bfloat16)
-            stage[order, mine, lane : lane + size] = done
-            pos = b // (blocks // 2)
-            for k in range(SHIFT // quarter):
-                to_n = lax.rem(b, blocks // 2) * (SHIFT // quarter) + k
-                here = jnp.logical_and(pos == own_pos, spot == to_n)
-
-                @pl.when(here)
-                def _():
-                    out_ref[:, res_cols(slot, spot)] = done[k * quarter : (k + 1) * quarter]
-
-                @pl.when(jnp.logical_not(here))
-                def _():
-                    result(slot, pos, to_n).start()
-
         def multiply_these(slot, first, count):
             @pl.loop(0, count)
             def _(k):
                 multiply(slot, lax.rem(first + k, blocks))
 
-        def near_wo(c):
-            o_mid_recv(0, c).wait_recv()
-            o_y(0, c, y).start()
-
-        def far_wo(c):
-            o_mid_recv(1, c).wait_recv()
-            o_y(1, c, y).start()
-
-        def pass_wo(c):
-            o_end(0, c).wait_recv()
-            o_mid_send(1, c).start()
+        def multiply_own(slot, b):
+            @pl.when(b // (blocks // 2) == own_pos)
+            def _():
+                multiply(slot, b)
+
+        def relay_wo(arrival, *onward):
+            def act(i):
+                @pl.loop(i * sub, (i + 1) * sub)
+                def _(c):
+                    arrival(c).wait_recv()
+                    for copy in onward:
+                        copy(c).start()
+
+            return act
+
+        near_wo = relay_wo(lambda c: o_mid_recv(0, c), lambda c: o_y(0, c, y))
+        far_wo = relay_wo(lambda c: o_mid_recv(1, c), lambda c: o_y(1, c, y))
+        pass_wo = relay_wo(lambda c: o_end(0, c), lambda c: o_mid_send(1, c))
+
+        def own_mid(first, last):
+            @pl.loop(first * sub, last * sub)
+            def _(c):
+                o_mid_send(0, c).start()
+
+        def half_of(shard, lane_half):
+            return wo_buf.at[shard, opp, :, lane_half * wo_lanes : (lane_half + 1) * wo_lanes]
 
         def last_y(c):
             w_y(1, c, opp).wait_recv()
@@ -874,8 +953,7 @@
             add_all(outer, opp, c)
 
         settle(0)
-        for c in range(3):
-            o_mid_send(0, c).start()
+        own_mid(0, 3)
         attend(0, 1)
         last_y(row_chunks)
         attend(0, 2)
@@ -896,105 +974,67 @@
         last_end(chunks - 1)
         last_y(row_chunks + 3)
         settle(1)
-        o_mid_send(0, 3).start()
+        own_mid(3, 4)
         attend(1, 1)
-        relay(0, 0)
         near_wo(0)
         near_wo(1)
+        relay(0, 0)
         attend(1, 2)
         near_wo(2)
         pass_wo(0)
         attend(1, 3)
         pass_wo(1)
-        own[heads + 1].wait()
-        own[heads + 2].wait()
+        for h in range(2):
+            own_wo(h).wait()
         relay(1, 1)
         gathered(1)
-        multiply(0, 1)
+        multiply_own(0, 1)
         kv_copy(1).wait_recv()
         attend(1, 0)
+        near_wo(3)
         relay(1, 2)
         gathered(2)
-        multiply(0, 2)
-        near_wo(3)
-        for j in range(2):
-            o_end(1, j).wait_recv()
-        multiply_these(2, 1, 2)
+        multiply_own(0, 2)
+        arrived(4, half_of(outer, 0))
+        multiply(2, own_pos + 1)
+        far_wo(0)
         relay(1, 3)
+        pass_wo(2)
         gathered(3)
-        multiply(0, 3)
-        multiply(2, 3)
-        pass_wo(2)
-
-        @pl.loop(0, wo_chunks)
-        def _(c):
-            o_y(0, c, opp).wait_recv()
-
-        multiply_these(1, 1, 3)
+        multiply_own(0, 3)
+        multiply_own(2, 3)
+        relay(1, 0)
+        far_wo(1)
         pass_wo(3)
-        far_wo(0)
-        relay(1, 0)
+        arrived(1, wo_buf.at[far_inner, opp])
+        multiply(1, side + 1)
+        multiply(1, 3)
         gathered(0)
-        multiply(0, 0)
-        far_wo(1)
         multiply(1, 0)
-        multiply(2, 0)
         far_wo(2)
+        multiply(1, own_pos + 1)
+        multiply_own(0, 0)
+        multiply_own(2, 0)
         far_wo(3)
         first = side * (blocks // 2)
-        for j in range(2):
-            o_y(1, j, opp).wait_recv()
+        arrived(2, half_of(far_outer, 0))
         multiply_these(4, first, blocks)
-        for j in range(2):
-            o_end(1, 2 + j).wait_recv()
-        multiply_these(3, first, blocks)
-        for j in range(2):
-            o_y(1, 2 + j, opp).wait_recv()
+        arrived(5, half_of(outer, 1))
+        multiply_these(3, own_pos * (blocks // 2), blocks // 2)
+        arrived(3, half_of(far_outer, 1))
         multiply_these(5, first, blocks)
 
-        for slot in range(len(slots)):
-            for p in range(narrow):
-                @pl.when(spot != p)
-                def _():
-                    result_arrival(slot, p).wait_recv()
-
-        @pl.loop(0, n)
-        def _(k):
-            h_x(k, spot).wait_send()
-            h_core(0, k, spot).wait_send()
-            h_core(1, k, x_n).wait_send()
-
-        @pl.loop(0, chunks)
-        def _(c):
-            for s in range(2):
-                w_mid_send(s, c).wait_send()
-                w_y(s, c, y).wait_send()
-
-        @pl.loop(direct, row_chunks)
-        def _(c):
-            w_y(2, c, y).wait_send()
-
-        @pl.loop(0, wo_chunks)
-        def _(c):
-            for s in range(2):
-                o_mid_send(s, c).wait_send()
-                o_y(s, c, y).wait_send()
-
-        for g in range(2):
-            kv_copy(g).wait_send()
-
-            @pl.loop(0, blocks)
-            def _(b):
-                att_x(g, b, spot).wait_send()
-                att_core(0, g, b, spot).wait_send()
-                att_core(1, g, b, x_n).wait_send()
-
-        for slot in range(len(slots)):
-            for pos in range(2):
-                for to_n in range(narrow):
-                    @pl.when(jnp.logical_not(jnp.logical_and(pos == own_pos, spot == to_n)))
-                    def _():
-                        result(slot, pos, to_n).wait_send()
+        sent(0, hid.at[pl.ds(0, 3 * quarter)])
+        sent(1, wbuf.at[pl.ds(0, 2)])
+        sent(2, wbuf.at[0, :, pl.ds(0, (row_chunks - direct) * rows)])
+        sent(3, kv_buf.at[:, :, pl.ds(0, SHIFT)])
+        sent(4, wo_buf.at[pl.ds(0, 2)])
+        sent(5, wo_buf.at[0, 0])
+        sent(6, att.at[pl.ds(0, 3)])
+        sent(7, att.at[0, 0])
+        pieces = 4 * (narrow - 1) + 2 * narrow
+        sent(8, hid.at[pl.ds(0, pieces * quarter * wo_cols // hid.shape[1])])
+        arrived(7, out_ref.at[:, pl.ds(0, 4 * (narrow - 1) * wo_cols)])
 
 
 def hub_layer(hidden, wq, wo, seg, shift_heads):
@@ -1002,7 +1042,7 @@
     tok, width = hidden.shape
     heads = wq.shape[2] // HEAD_DIM
     row_chunks = wq.shape[1] // HUB_ROWS
-    chunks, wo_chunks = 2 * row_chunks, 4
+    chunks, wo_chunks = 2 * row_chunks, 8
     cols = wo.shape[1]
     wo_half, wo_cols = wo.shape[0] // 2, cols // narrow
     quarter, span = tok // narrow, 2 * tok
@@ -1027,17 +1067,14 @@
             pltpu.VMEM((n, 2, wo_half, wo_cols), bf16),
             pltpu.VMEM((n, span, wo_cols), bf16),
             pltpu.VMEM((span, seg.shape[1]), jnp.int32),
-            dma((heads + 3,)),
+            dma((4,)),
+            dma((9,)),
+            dma((8 + blocks,)),
         ]
-        + [dma((n,))] * 4
-        + [dma((2, n))] * 2
-        + [dma((2, chunks))] * 4
-        + [dma((3, chunks))] * 2
-        + [dma((2, 2))]
-        + [dma((2, wo_chunks))] * 6
-        + [dma((2, blocks))] * 2
-        + [dma((2, 2, blocks))] * 2
-        + [dma((6, 2, narrow)), dma((6, narrow))],
+        + [dma((n,))] * 2
+        + [dma((2, chunks))] * 3
+        + [dma((row_chunks,)), dma((2,)), dma((2, wo_chunks)), dma((wo_chunks,)), dma((wo_chunks,))]
+        + [dma((2, blocks))] * 2,
         compiler_params=pltpu.CompilerParams(
             collective_id=0, has_side_effects=True, vmem_limit_bytes=58 * 1024 * 1024
         ),

time: 131 us -> 126 us (0.962)
  Pallas kernels: 129 us -> 125 us
    pallas_call x1, Pallas kernels: 129 us -> 125 us  [hub_layer(): pl.pallas_call(functools.partial(hub_kernel, row_chunks, DIRECT), out_sha...]
where the time goes in v5:
time: 126 us
  Pallas kernels  125 us (99%)
    pallas_call x1, Pallas kernels, hub_layer(): pl.pallas_call(functools.partial(hub_kernel, row_chunks, DIRECT), out_sha...  125 us

profile of v5, /device:TPU:1, one launch (start us, length us, event | category | flops | bytes accessed | tf_op | source)
XLA Modules:
  0.0 125.8 jit_solution(12306761612229310744)
XLA Ops:
  0.0 124.8 %shard_map.55 = bf16[128,4096]{1,0:T(8,128)(2,1)S(1)} custom-call(bf16[512,4096]{1,0:T(8,128)(2,1)} %hidden_ref.1, bf16[3,1024,512]{2,1,0:T(8,128)(2,1)} %bitcast.2, bf16[2048,1024]{1,0:T(8,128)(2,1)} %wo_ref.1, s32[16,128]{1,0:T(8,128)} %bitcast.3, s32[16]{0:T(128)} %shift_ref.1), custom_call_target="tpu_custom_call" | custom-call | tf_op jit(solution)/shard_map/pallas_call | solution.py:1055
  124.8 1.0 copy.7

commit v6 on v5

--- a/solution.py
+++ b/solution.py
@@ -432,7 +432,7 @@
 def hub_kernel(
     row_chunks, direct,
     hidden_ref, wq_ref, wo_ref, seg_ref, shift_ref, out_ref,
-    wbuf, hid, acc, q_buf, kv_buf, att, wo_buf, stage, seg_col,
+    wbuf, hid, acc, q_buf, kv_buf, att, wo_buf, stage, early, seg_col,
     own_sem, sends, joint, he_r, hx_r, wm_r, we_r, wy_r, w0_r, kv_r, om_r, oe_r, od_r, ax_r, ae_r,
 ):
     n, narrow = lax.axis_size("wide"), lax.axis_size("narrow")
@@ -540,7 +540,7 @@
 
     def o_end(j, c):
         part = y if j == 0 else opp
-        return remote(wo_at(part, c), o_at(outer, part, c), sends.at[4], oe_r.at[c] if j == 0 else joint.at[4 + c // (2 * sub)], to_inner)
+        return remote(wo_at(part, c), o_at(outer, part, c), sends.at[4], oe_r.at[c] if j == 0 else joint.at[4], to_inner)
 
     def o_mid_send(s, c):
         if s == 0:
@@ -602,20 +602,26 @@
             {"wide": side * (n // 2) + pos, "narrow": to_n},
         )
 
-    def multiply(slot, b):
+    def product(slot, b, firsts):
         order, lane, size = slots[slot]
         mine = pl.ds(pl.multiple_of(b * SHIFT, SHIFT), SHIFT)
         a_cols = att.shape[3]
         total = None
-        for p in range(narrow):
-            for g in range(2):
-                start = (p % (narrow // 2) * 2 + g) * a_cols
-                term = jnp.dot(
-                    att[p, g, mine],
-                    wo_buf[shards[order], p // (narrow // 2), start : start + a_cols, lane : lane + size],
-                    preferred_element_type=jnp.float32,
-                )
-                total = term if total is None else total + term
+        for row_half in firsts:
+            for p in range(narrow // 2):
+                for g in range(2):
+                    start = (p * 2 + g) * a_cols
+                    term = jnp.dot(
+                        att[row_half * (narrow // 2) + p, g, mine],
+                        wo_buf[shards[order], row_half, start : start + a_cols, lane : lane + size],
+                        preferred_element_type=jnp.float32,
+                    )
+                    total = term if total is None else total + term
+        return total
+
+    def emit(slot, b, total):
+        order, lane, size = slots[slot]
+        mine = pl.ds(pl.multiple_of(b * SHIFT, SHIFT), SHIFT)
         done = total.astype(jnp.bfloat16)
         stage[order, mine, lane : lane + size] = done
         pos = b // (blocks // 2)
@@ -631,6 +637,9 @@
             def _():
                 result(slot, pos, to_n).start()
 
+    def multiply(slot, b):
+        emit(slot, b, product(slot, b, (0, 1)))
+
     def kv_copy(g):
         return remote(
             kv_buf.at[pl.ds(2 * g, 2), :, pl.ds(span, SHIFT)], kv_buf.at[pl.ds(2 * g, 2), :, pl.ds(0, SHIFT)],
@@ -674,11 +683,10 @@
             def _(c):
                 act(w_end(1, c))
 
-            for lane_half in range(2):
-                for j in range(2):
-                    @pl.loop(lane_half * 2 * sub, (lane_half + 1) * 2 * sub)
-                    def _(c):
-                        act(o_end(j, c))
+            for j in range(2):
+                @pl.loop(0, wo_chunks)
+                def _(c):
+                    act(o_end(j, c))
 
         each_end(lambda copy: copy.start())
         for h in range(2):
@@ -797,6 +805,11 @@
         def _(u):
             add(own_row, tok, inner, u // chunks, lax.rem(u, chunks))
 
+        def own_mid(first, last):
+            @pl.loop(first, last)
+            def _(c):
+                o_mid_send(0, c).start()
+
         lag = row_chunks
         lead = chunks - 2
         catch_up = 4 * chunks - lag
@@ -832,6 +845,10 @@
             @pl.when(t == chunks)
             def _():
                 arrived(0, hid.at[pl.ds(far_row, narrow // 2 * quarter)])
+
+            @pl.when(t == lead + chunks)
+            def _():
+                own_mid(0, 2)
 
             add_at(t, far_shard(s), y, c)
 
@@ -923,8 +940,8 @@
                 multiply(slot, b)
 
         def relay_wo(arrival, *onward):
-            def act(i):
-                @pl.loop(i * sub, (i + 1) * sub)
+            def act(i, count):
+                @pl.loop(i, i + count)
                 def _(c):
                     arrival(c).wait_recv()
                     for copy in onward:
@@ -936,11 +953,6 @@
         far_wo = relay_wo(lambda c: o_mid_recv(1, c), lambda c: o_y(1, c, y))
         pass_wo = relay_wo(lambda c: o_end(0, c), lambda c: o_mid_send(1, c))
 
-        def own_mid(first, last):
-            @pl.loop(first * sub, last * sub)
-            def _(c):
-                o_mid_send(0, c).start()
-
         def half_of(shard, lane_half):
             return wo_buf.at[shard, opp, :, lane_half * wo_lanes : (lane_half + 1) * wo_lanes]
 
@@ -953,9 +965,10 @@
             add_all(outer, opp, c)
 
         settle(0)
-        own_mid(0, 3)
+        own_mid(2, 7)
         attend(0, 1)
         last_y(row_chunks)
+        near_wo(0, 2)
         attend(0, 2)
         last_y(row_chunks + 1)
         attend(0, 3)
@@ -970,59 +983,65 @@
         relay(0, 2)
         last_y(row_chunks + 2)
         last_end(chunks - 2)
+        near_wo(2, 2)
         relay(0, 3)
         last_end(chunks - 1)
         last_y(row_chunks + 3)
         settle(1)
-        own_mid(3, 4)
+        own_mid(7, 8)
         attend(1, 1)
-        near_wo(0)
-        near_wo(1)
+        near_wo(4, 2)
+        attend(1, 2)
         relay(0, 0)
-        attend(1, 2)
-        near_wo(2)
-        pass_wo(0)
+        pass_wo(0, 2)
         attend(1, 3)
-        pass_wo(1)
+        near_wo(6, 1)
         for h in range(2):
             own_wo(h).wait()
+        pass_wo(2, 2)
         relay(1, 1)
         gathered(1)
         multiply_own(0, 1)
+        pass_wo(4, 2)
         kv_copy(1).wait_recv()
         attend(1, 0)
-        near_wo(3)
+        near_wo(7, 1)
+        pass_wo(6, 2)
         relay(1, 2)
         gathered(2)
         multiply_own(0, 2)
-        arrived(4, half_of(outer, 0))
-        multiply(2, own_pos + 1)
-        far_wo(0)
+        far_wo(0, 2)
         relay(1, 3)
-        pass_wo(2)
         gathered(3)
         multiply_own(0, 3)
-        multiply_own(2, 3)
-        relay(1, 0)
-        far_wo(1)
-        pass_wo(3)
         arrived(1, wo_buf.at[far_inner, opp])
         multiply(1, side + 1)
+        far_wo(2, 1)
+        relay(1, 0)
         multiply(1, 3)
+        far_wo(3, 2)
         gathered(0)
         multiply(1, 0)
-        far_wo(2)
+        far_wo(5, 1)
         multiply(1, own_pos + 1)
         multiply_own(0, 0)
-        multiply_own(2, 0)
-        far_wo(3)
         first = side * (blocks // 2)
+        far_wo(6, 2)
         arrived(2, half_of(far_outer, 0))
         multiply_these(4, first, blocks)
-        arrived(5, half_of(outer, 1))
-        multiply_these(3, own_pos * (blocks // 2), blocks // 2)
+        arrived(4, wo_buf.at[outer, opp])
+        multiply_these(6, own_pos * (blocks // 2), blocks // 2)
+
+        @pl.loop(0, blocks)
+        def _(b):
+            early[b] = product(5, b, (y,))
+
         arrived(3, half_of(far_outer, 1))
-        multiply_these(5, first, blocks)
+
+        @pl.loop(0, blocks)
+        def _(turn):
+            b = lax.rem(first + turn, blocks)
+            emit(5, b, early[b] + product(5, b, (opp,)))
 
         sent(0, hid.at[pl.ds(0, 3 * quarter)])
         sent(1, wbuf.at[pl.ds(0, 2)])
@@ -1066,6 +1085,7 @@
             pltpu.VMEM((narrow, 2, span, 2 * HEAD_DIM), bf16),
             pltpu.VMEM((n, 2, wo_half, wo_cols), bf16),
             pltpu.VMEM((n, span, wo_cols), bf16),
+            pltpu.VMEM((blocks, SHIFT, wo_cols // 2), jnp.float32),
             pltpu.VMEM((span, seg.shape[1]), jnp.int32),
             dma((4,)),
             dma((9,)),

time: 126 us -> 125 us (level)
  Pallas kernels: 125 us -> 123 us
    pallas_call x1, Pallas kernels: 125 us -> 123 us  [hub_layer(): pl.pallas_call(functools.partial(hub_kernel, row_chunks, DIRECT), out_sha...]
where the time goes in v6:
time: 125 us; the launch traced here: 124 us
  Pallas kernels  123 us (98%)
    pallas_call x1, Pallas kernels, hub_layer(): pl.pallas_call(functools.partial(hub_kernel, row_chunks, DIRECT), out_sha...  123 us

profile of v6, /device:TPU:1, one launch (start us, length us, event | category | flops | bytes accessed | tf_op | source)
XLA Modules:
  0.0 124.4 jit_solution(7178370403936529284)
XLA Ops:
  0.0 123.4 %shard_map.55 = bf16[128,4096]{1,0:T(8,128)(2,1)S(1)} custom-call(bf16[512,4096]{1,0:T(8,128)(2,1)} %hidden_ref.1, bf16[3,1024,512]{2,1,0:T(8,128)(2,1)} %bitcast.2, bf16[2048,1024]{1,0:T(8,128)(2,1)} %wo_ref.1, s32[16,128]{1,0:T(8,128)} %bitcast.3, s32[16]{0:T(128)} %shift_ref.1), custom_call_target="tpu_custom_call" | custom-call | tf_op jit(solution)/shard_map/pallas_call | solution.py:1074
  123.4 1.0 copy.7

commit v7 on v6

--- a/solution.py
+++ b/solution.py
@@ -540,12 +540,16 @@
 
     def o_end(j, c):
         part = y if j == 0 else opp
-        return remote(wo_at(part, c), o_at(outer, part, c), sends.at[4], oe_r.at[c] if j == 0 else joint.at[4], to_inner)
+        return remote(wo_at(part, c), o_at(outer, part, c), sends.at[4], oe_r.at[c] if j == 0 else joint.at[4 + c // 4 * (1 + 7 * lax.rem(c // 2, 2))], to_inner)
 
     def o_mid_send(s, c):
         if s == 0:
             return remote(wo_at(y, c), o_at(inner, y, c), sends.at[4], om_r.at[s, c], to_far)
         return remote(o_at(outer, y, c), o_at(outer, y, c), sends.at[4], om_r.at[s, c], to_far)
+
+    def o_mid_direct(c):
+        ref = o_at(outer, opp, c)
+        return remote(ref, ref, sends.at[4], joint.at[13], to_far)
 
     def o_mid_recv(s, c):
         ref = o_at(far_shard(s), y, c)
@@ -683,8 +687,8 @@
             def _(c):
                 act(w_end(1, c))
 
-            for j in range(2):
-                @pl.loop(0, wo_chunks)
+            for j, from_c, to_c in ((0, 0, wo_chunks), (1, 6, 8), (1, 4, 6), (1, 0, 4)):
+                @pl.loop(from_c, to_c)
                 def _(c):
                     act(o_end(j, c))
 
@@ -956,6 +960,9 @@
         def half_of(shard, lane_half):
             return wo_buf.at[shard, opp, :, lane_half * wo_lanes : (lane_half + 1) * wo_lanes]
 
+        def corner(shard, row):
+            return wo_buf.at[shard, opp, row * 2 * wo_rows : (row + 1) * 2 * wo_rows, wo_lanes:]
+
         def last_y(c):
             w_y(1, c, opp).wait_recv()
             add_all(far_outer, opp, c)
@@ -968,7 +975,6 @@
         own_mid(2, 7)
         attend(0, 1)
         last_y(row_chunks)
-        near_wo(0, 2)
         attend(0, 2)
         last_y(row_chunks + 1)
         attend(0, 3)
@@ -983,11 +989,12 @@
         relay(0, 2)
         last_y(row_chunks + 2)
         last_end(chunks - 2)
-        near_wo(2, 2)
         relay(0, 3)
         last_end(chunks - 1)
+        near_wo(0, 2)
         last_y(row_chunks + 3)
         settle(1)
+        near_wo(2, 2)
         own_mid(7, 8)
         attend(1, 1)
         near_wo(4, 2)
@@ -1021,27 +1028,38 @@
         multiply(1, 3)
         far_wo(3, 2)
         gathered(0)
+        arrived(12, corner(outer, 1))
+        for c in range(wo_chunks - 2, wo_chunks):
+            o_mid_direct(c).start()
         multiply(1, 0)
         far_wo(5, 1)
         multiply(1, own_pos + 1)
         multiply_own(0, 0)
         first = side * (blocks // 2)
-        far_wo(6, 2)
+        arrived(5, corner(outer, 0))
+        multiply_these(3, own_pos * (blocks // 2), blocks // 2)
         arrived(2, half_of(far_outer, 0))
         multiply_these(4, first, blocks)
-        arrived(4, wo_buf.at[outer, opp])
-        multiply_these(6, own_pos * (blocks // 2), blocks // 2)
+        for c in range(wo_chunks - 2, wo_chunks):
+            o_mid_recv(1, c).wait_recv()
 
         @pl.loop(0, blocks)
         def _(b):
             early[b] = product(5, b, (y,))
 
-        arrived(3, half_of(far_outer, 1))
-
-        @pl.loop(0, blocks)
-        def _(turn):
-            b = lax.rem(first + turn, blocks)
-            emit(5, b, early[b] + product(5, b, (opp,)))
+        arrived(3, corner(far_outer, 0))
+        arrived(13, corner(far_outer, 1))
+
+        def last_piece(begin):
+            @pl.loop(0, blocks // 2)
+            def _(turn):
+                b = begin + turn
+                emit(5, b, early[b] + product(5, b, (opp,)))
+
+        last_piece(first)
+        arrived(4, half_of(outer, 0))
+        multiply_these(2, own_pos * (blocks // 2), blocks // 2)
+        last_piece(own_pos * (blocks // 2))
 
         sent(0, hid.at[pl.ds(0, 3 * quarter)])
         sent(1, wbuf.at[pl.ds(0, 2)])
@@ -1089,7 +1107,7 @@
             pltpu.VMEM((span, seg.shape[1]), jnp.int32),
             dma((4,)),
             dma((9,)),
-            dma((8 + blocks,)),
+            dma((10 + blocks,)),
         ]
         + [dma((n,))] * 2
         + [dma((2, chunks))] * 3

time: 125 us -> 125 us (level)
  no operation moved by 1% of the time
where the time goes in v7:
time: 125 us; the launch traced here: 124 us
  Pallas kernels  123 us (98%)
    pallas_call x1, Pallas kernels, hub_layer(): pl.pallas_call(functools.partial(hub_kernel, row_chunks, DIRECT), out_sha...  123 us

profile of v7, /device:TPU:1, one launch (start us, length us, event | category | flops | bytes accessed | tf_op | source)
XLA Modules:
  0.0 124.5 jit_solution(8717313959583587727)
XLA Ops:
  0.0 123.5 %shard_map.55 = bf16[128,4096]{1,0:T(8,128)(2,1)S(1)} custom-call(bf16[512,4096]{1,0:T(8,128)(2,1)} %hidden_ref.1, bf16[3,1024,512]{2,1,0:T(8,128)(2,1)} %bitcast.2, bf16[2048,1024]{1,0:T(8,128)(2,1)} %wo_ref.1, s32[16,128]{1,0:T(8,128)} %bitcast.3, s32[16]{0:T(128)} %shift_ref.1), custom_call_target="tpu_custom_call" | custom-call | tf_op jit(solution)/shard_map/pallas_call | solution.py:1092
  123.5 1.0 copy.7

commit v8 on v7

--- a/solution.py
+++ b/solution.py
@@ -431,8 +431,8 @@
 
 def hub_kernel(
     row_chunks, direct,
-    hidden_ref, wq_ref, wo_ref, seg_ref, shift_ref, out_ref,
-    wbuf, hid, acc, q_buf, kv_buf, att, wo_buf, stage, early, seg_col,
+    hidden_ref, wq_ref, wo_ref, seg_hbm, shift_hbm, out_ref,
+    wbuf, hid, acc, q_buf, kv_buf, att, wo_buf, stage, early, seg_col, seg_ref, shift_ref,
     own_sem, sends, joint, he_r, hx_r, wm_r, we_r, wy_r, w0_r, kv_r, om_r, oe_r, od_r, ax_r, ae_r,
 ):
     n, narrow = lax.axis_size("wide"), lax.axis_size("narrow")
@@ -753,7 +753,11 @@
             for h in range(heads)
         ]
         own.append(pltpu.make_async_copy(hidden_ref, hid.at[pl.ds(own_row, tok)], own_sem.at[1]))
-        for copy in own:
+        small = [
+            pltpu.make_async_copy(seg_hbm, seg_ref, own_sem.at[4]),
+            pltpu.make_async_copy(shift_hbm, shift_ref, own_sem.at[5]),
+        ]
+        for copy in own + small:
             copy.start()
         for h in range(2):
             own_wo(h).start()
@@ -768,6 +772,8 @@
             o_down(c).start()
 
         acc[...] = jnp.zeros_like(acc)
+        for copy in small:
+            copy.wait()
         seg_rows = seg_ref.shape[0]
         lanes = seg_ref.shape[1]
         seg_first = side * (span // lanes)
@@ -1085,14 +1091,13 @@
     quarter, span = tok // narrow, 2 * tok
     blocks = span // SHIFT
     vmem = pl.BlockSpec(memory_space=pltpu.VMEM)
-    smem = pl.BlockSpec(memory_space=pltpu.SMEM)
     hbm = pl.BlockSpec(memory_space=pl.ANY)
     dma = pltpu.SemaphoreType.DMA
     bf16 = jnp.bfloat16
     return pl.pallas_call(
         functools.partial(hub_kernel, row_chunks, DIRECT),
         out_shape=pltpu.VMEM((quarter, n * cols), bf16),
-        in_specs=[hbm, hbm, hbm, vmem, smem],
+        in_specs=[hbm] * 5,
         out_specs=vmem,
         scratch_shapes=[
             pltpu.VMEM((heads, 3, width, HEAD_DIM), bf16),
@@ -1105,7 +1110,9 @@
             pltpu.VMEM((n, span, wo_cols), bf16),
             pltpu.VMEM((blocks, SHIFT, wo_cols // 2), jnp.float32),
             pltpu.VMEM((span, seg.shape[1]), jnp.int32),
-            dma((4,)),
+            pltpu.VMEM(seg.shape, jnp.int32),
+            pltpu.SMEM(shift_heads.shape, jnp.int32),
+            dma((6,)),
             dma((9,)),
             dma((10 + blocks,)),
         ]

time: 125 us -> 124 us (level)
  no operation moved by 1% of the time
where the time goes in v8:
time: 124 us
  Pallas kernels  123 us (99%)
    pallas_call x1, Pallas kernels, hub_layer(): pl.pallas_call(functools.partial(hub_kernel, row_chunks, DIRECT), out_sha...  123 us

profile of v8, /device:TPU:1, one launch (start us, length us, event | category | flops | bytes accessed | tf_op | source)
XLA Modules:
  0.0 123.6 jit_solution(15908040312500156498)
XLA Ops:
  0.0 122.6 %shard_map.55 = bf16[128,4096]{1,0:T(8,128)(2,1)S(1)} custom-call(bf16[512,4096]{1,0:T(8,128)(2,1)} %hidden_ref.1, bf16[3,1024,512]{2,1,0:T(8,128)(2,1)} %bitcast.2, bf16[2048,1024]{1,0:T(8,128)(2,1)} %wo_ref.1, s32[16,128]{1,0:T(8,128)} %bitcast.3, s32[16]{0:T(128)} %shift_hbm.1), custom_call_target="tpu_custom_call" | custom-call | tf_op jit(solution)/shard_map/pallas_call | solution.py:1097
  122.6 1.0 copy.7
